TPU v7x, 256 devices: a whole 4x4x8 slice. The times are simulated.
256 devices in a mesh: row: 32 (over x, z), col: 8 (over y, core).
Axes of the slice: x: 4, y: 4, z: 8, core: 2. Of those that a mesh axis runs over, the one named last changes fastest.
Arguments:
- panel_block: float32 [16384, 128], P('row'), may hold values from -8 to 8, as said below
- trailing: float32 [16384, 16384], P('row', 'col'), may hold values from -80 to 80
Outputs:
- reduced: float32 [16384, 16384], P('row', 'col')
- band_block: float32 [128, 128], replicated
- first_factor: float32 [128, 128], replicated
Inputs may be any that keep to these rules, and one draw needn't show every extreme that they name: `panel_block`: entries of order the inverse square root of 16384; rows may differ in scale; the columns may be nearly dependent, with a condition number of the panel up to a few thousand; the first 128 rows of the orthonormal basis have spectral norm at most 0.8, so that I + top^T needs no pivoting.
All inputs are finite; a program needn't handle non-finite values.
Results may differ from a plain program's by a relative error of at most 0.0017.
Values sent between devices are 32-bit elements; how exact they have to be, the bound alone decides.
A program may use at most 128 MiB of HBM per device.

v0:
```python
import jax
import jax.numpy as jnp
from jax import lax
from jax.sharding import PartitionSpec as P

HIGH = lax.Precision.HIGHEST


def broadcast(shard, axis, root):
    mine = lax.axis_index(axis) == root
    return lax.psum(jnp.where(mine, shard, jnp.zeros_like(shard)), axis)


def gram_of(values):
    return lax.dot_general(
        values, values, (((0,), (0,)), ((), ())), precision=HIGH, preferred_element_type=jnp.float32
    )


def times_of(left, right):
    return jnp.dot(left, right, precision=HIGH, preferred_element_type=jnp.float32)


def outer_of(left, right):
    return lax.dot_general(
        left, right, (((1,), (1,)), ((), ())), precision=HIGH, preferred_element_type=jnp.float32
    )


def gram_both(left, right):
    return lax.dot_general(
        left, right, (((0,), (0,)), ((), ())), precision=HIGH, preferred_element_type=jnp.float32
    )


def eliminate_small(square):
    size_n = square.shape[0]
    augmented = jnp.concatenate([square, jnp.eye(size_n, dtype=square.dtype)], axis=1)
    positions = jnp.arange(size_n)

    def eliminate(pivot, current):
        pivot_row = lax.dynamic_index_in_dim(current, pivot, 0, keepdims=False)
        pivot_row = pivot_row / pivot_row[pivot]
        column = lax.dynamic_index_in_dim(current, pivot, 1, keepdims=False)
        column = column - (positions == pivot).astype(current.dtype)
        return current - column[:, None] * pivot_row[None, :]

    augmented = lax.fori_loop(0, size_n, eliminate, augmented)
    return augmented[:, size_n:]


def invert_square(square):
    size_n = square.shape[0]
    if size_n <= 16:
        return eliminate_small(square)
    half = size_n // 2
    upper_left = square[:half, :half]
    upper_right = square[:half, half:]
    lower_left = square[half:, :half]
    lower_right = square[half:, half:]
    left_inverse = invert_square(upper_left)
    left_times_right = times_of(left_inverse, upper_right)
    lower_times_left = times_of(lower_left, left_inverse)
    schur = lower_right - times_of(lower_left, left_times_right)
    schur_inverse = invert_square(schur)
    top_right = -times_of(left_times_right, schur_inverse)
    bottom_left = -times_of(schur_inverse, lower_times_left)
    top_left = left_inverse - times_of(top_right, lower_times_left)
    upper = jnp.concatenate([top_left, top_right], axis=1)
    lower = jnp.concatenate([bottom_left, schur_inverse], axis=1)
    return jnp.concatenate([upper, lower], axis=0)


def right_solve(factor, values):
    return lax.linalg.triangular_solve(
        factor, values, left_side=False, lower=True, transpose_a=True
    )


def body(panel_block, trailing):
    shard_rows = panel_block.shape[0]
    panel_width = panel_block.shape[1]
    col_count = trailing.shape[1]
    row_index = lax.axis_index("row")
    col_index = lax.axis_index("col")
    first_gram = lax.psum(gram_of(panel_block), "row")
    first_factor = jnp.linalg.cholesky(first_gram)
    first_basis = right_solve(first_factor, panel_block)
    second_gram = lax.psum(gram_of(first_basis), "row")
    second_factor = jnp.linalg.cholesky(second_gram)
    basis = right_solve(second_factor, first_basis)
    top_basis = broadcast(basis[:panel_width], "row", 0)
    band_block = -times_of(second_factor.T, first_factor.T)
    kernel = invert_square(jnp.eye(panel_width, dtype=jnp.float32) + top_basis.T)
    global_rows = row_index * shard_rows + jnp.arange(shard_rows)
    ident = (global_rows[:, None] == jnp.arange(panel_width)[None, :]).astype(jnp.float32)
    vectors = basis + ident
    all_vectors = lax.all_gather(vectors, "row", axis=0, tiled=True)
    col_vectors = lax.dynamic_slice_in_dim(all_vectors, col_index * col_count, col_count, 0)
    partial_product = times_of(trailing, col_vectors)
    row_product = lax.psum(partial_product, "col")
    applied = times_of(row_product, kernel)
    inner_sum = lax.psum(gram_both(vectors, applied), "row")
    inner = times_of(kernel.T, inner_sum)
    row_update = applied - 0.5 * times_of(vectors, inner)
    all_update = lax.all_gather(row_update, "row", axis=0, tiled=True)
    col_update = lax.dynamic_slice_in_dim(all_update, col_index * col_count, col_count, 0)
    reduced = trailing - outer_of(vectors, col_update) - outer_of(row_update, col_vectors)
    return (reduced, band_block, first_factor)


def solution(mesh):
    in_specs = (P("row", None), P("row", "col"))
    out_specs = (P("row", "col"), P(), P())
    return jax.shard_map(body, mesh=mesh, in_specs=in_specs, out_specs=out_specs, check_vma=False)
```

profile of v0, /device:TPU:1, one launch (start us, length us, event | category | flops | bytes accessed | tf_op | source)
XLA Modules:
  0.0 1025.3 jit_solution(8369350252822602380)
XLA Ops:
  7.2 0.9 copy-done
  8.1 1.2 fusion.134
  9.4 143.5 %all-reduce.6.cloned.1.call-done = f32[128,128]{0,1:T(8,128)} async-done(((f32[128,128]{0,1:T(8,128)}), f32[128,128]{0,1:T(8,128)}) %all-reduce.6.cloned.1.call-update) | async-done | bytes 65552 | tf_op jit(solution)/shard_map/psum | solution.py:86
  152.9 0.9 copy.26
  153.9 0.9 fusion.57
  154.7 11.7 %cholesky.44 = f32[128,128]{1,0:T(8,128)S(1)} custom-call(f32[128,128]{1,0:T(8,128)S(1)} %fusion.57), custom_call_target="Cholesky" | custom-call | tf_op jit(solution)/shard_map/jit(cholesky)/cholesky | solution.py:87
  167.8 9.8 custom-call.6
  178.0 1.0 fusion.135
  179.3 139.5 %all-reduce.8.cloned.1.call-done = f32[128,128]{0,1:T(8,128)} async-done(((f32[128,128]{0,1:T(8,128)}), f32[128,128]{0,1:T(8,128)}) %all-reduce.8.cloned.1.call-update) | async-done | bytes 65552 | tf_op jit(solution)/shard_map/psum | solution.py:89
  318.8 0.9 copy.28
  319.7 0.9 fusion.55
  320.6 11.7 %cholesky.55 = f32[128,128]{1,0:T(8,128)S(1)} custom-call(f32[128,128]{1,0:T(8,128)S(1)} %fusion.55), custom_call_target="Cholesky" | custom-call | tf_op jit(solution)/shard_map/jit(cholesky)/cholesky | solution.py:90
  333.5 9.8 custom-call.7
  343.3 1.1 convert_add_fusion
  346.0 138.9 %all-reduce.12.cloned.1.call-done = f32[128,128]{1,0:T(8,128)} async-done(((f32[128,128]{1,0:T(8,128)}), f32[128,128]{1,0:T(8,128)}) %all-reduce.12.cloned.1.call-update) | async-done | bytes 65552 | tf_op jit(solution)/shard_map/psum | solution.py:11
  484.9 0.9 fusion.65
  485.9 24.0 %while.136 = (s32[]{:T(128)}, f32[16,32]{0,1:T(8,128)S(1)}, s32[]{:T(128)}, s32[]{:T(128)}, s32[]{:T(128)}, /*index=5*/s32[]{:T(128)}) while((s32[]{:T(128)}, f32[16,32]{0,1:T(8,128)S(1)}, s32[]{:T(128)}, s32[]{:T(128)}, s32[]{:T(128)}, /*index=5*/s32[]{:T(128)}) %tuple.325), condition=%wide.region_7.10_spmd.clone, body=%wide.region_6.9_spmd.clone.sunk | while | flops 1108 | bytes 5825 | solution.py:48
  501.5 0.8 fusion.206
  503.0 0.8 fusion.206
  506.0 0.8 fusion.206
  509.1 0.8 fusion.206
  510.8 24.0 %while.137 = (s32[]{:T(128)}, f32[16,32]{0,1:T(8,128)S(1)}, s32[]{:T(128)}, s32[]{:T(128)}, s32[]{:T(128)}, /*index=5*/s32[]{:T(128)}) while((s32[]{:T(128)}, f32[16,32]{0,1:T(8,128)S(1)}, s32[]{:T(128)}, s32[]{:T(128)}, s32[]{:T(128)}, /*index=5*/s32[]{:T(128)}) %tuple.328), condition=%wide.region_9.12_spmd.clone, body=%wide.region_8.11_spmd.clone.sunk | while | flops 1108 | bytes 5825 | solution.py:48
  515.8 0.8 fusion.208
  520.3 0.8 fusion.208
  521.8 0.8 fusion.208
  536.2 24.0 %while.138 = (s32[]{:T(128)}, f32[16,32]{0,1:T(8,128)S(1)}, s32[]{:T(128)}, s32[]{:T(128)}, s32[]{:T(128)}, /*index=5*/s32[]{:T(128)}) while((s32[]{:T(128)}, f32[16,32]{0,1:T(8,128)S(1)}, s32[]{:T(128)}, s32[]{:T(128)}, s32[]{:T(128)}, /*index=5*/s32[]{:T(128)}) %tuple.331), condition=%wide.region_11.14_spmd.clone, body=%wide.region_10.13_spmd.clone.sunk | while | flops 1108 | bytes 5825 | solution.py:48
  539.8 0.8 fusion.210
  541.3 0.8 fusion.210
  553.4 0.8 fusion.210
  556.4 0.8 fusion.210
  561.1 24.0 %while.139 = (s32[]{:T(128)}, f32[16,32]{0,1:T(8,128)S(1)}, s32[]{:T(128)}, s32[]{:T(128)}, s32[]{:T(128)}, /*index=5*/s32[]{:T(128)}) while((s32[]{:T(128)}, f32[16,32]{0,1:T(8,128)S(1)}, s32[]{:T(128)}, s32[]{:T(128)}, s32[]{:T(128)}, /*index=5*/s32[]{:T(128)}) %tuple.334), condition=%wide.region_13.16_spmd.clone, body=%wide.region_12.15_spmd.clone.sunk | while | flops 1108 | bytes 5825 | solution.py:48
  561.7 0.8 fusion.212
  567.7 0.8 fusion.212
  587.1 24.0 %while.140 = (s32[]{:T(128)}, f32[16,32]{0,1:T(8,128)S(1)}, s32[]{:T(128)}, s32[]{:T(128)}, s32[]{:T(128)}, /*index=5*/s32[]{:T(128)}) while((s32[]{:T(128)}, f32[16,32]{0,1:T(8,128)S(1)}, s32[]{:T(128)}, s32[]{:T(128)}, s32[]{:T(128)}, /*index=5*/s32[]{:T(128)}) %tuple.337), condition=%wide.region_15.18_spmd.clone, body=%wide.region_14.17_spmd.clone.sunk | while | flops 1108 | bytes 5825 | solution.py:48
  611.7 24.0 %while.141 = (s32[]{:T(128)}, f32[16,32]{0,1:T(8,128)S(1)}, s32[]{:T(128)}, s32[]{:T(128)}, s32[]{:T(128)}, /*index=5*/s32[]{:T(128)}) while((s32[]{:T(128)}, f32[16,32]{0,1:T(8,128)S(1)}, s32[]{:T(128)}, s32[]{:T(128)}, s32[]{:T(128)}, /*index=5*/s32[]{:T(128)}) %tuple.340), condition=%wide.region_17.20_spmd.clone, body=%wide.region_16.19_spmd.clone.sunk | while | flops 1108 | bytes 5825 | solution.py:48
  637.1 24.0 %while.142 = (s32[]{:T(128)}, f32[16,32]{0,1:T(8,128)S(1)}, s32[]{:T(128)}, s32[]{:T(128)}, s32[]{:T(128)}, /*index=5*/s32[]{:T(128)}) while((s32[]{:T(128)}, f32[16,32]{0,1:T(8,128)S(1)}, s32[]{:T(128)}, s32[]{:T(128)}, s32[]{:T(128)}, /*index=5*/s32[]{:T(128)}) %tuple.343), condition=%wide.region_19.22_spmd.clone, body=%wide.region_18.21_spmd.clone.sunk | while | flops 1108 | bytes 5825 | solution.py:48
  661.7 24.0 %while.143 = (s32[]{:T(128)}, f32[16,32]{0,1:T(8,128)S(1)}, s32[]{:T(128)}, s32[]{:T(128)}, s32[]{:T(128)}, /*index=5*/s32[]{:T(128)}) while((s32[]{:T(128)}, f32[16,32]{0,1:T(8,128)S(1)}, s32[]{:T(128)}, s32[]{:T(128)}, s32[]{:T(128)}, /*index=5*/s32[]{:T(128)}) %tuple.346), condition=%wide.region_21.24_spmd.clone, body=%wide.region_20.23_spmd.clone.sunk | while | flops 1108 | bytes 5825 | solution.py:48
  688.1 7.6 convolution_bitcast_fusion
  696.0 65.7 %all-reduce.10.cloned.1.call-done = f32[512,128]{0,1:T(8,128)} async-done(((f32[512,128]{0,1:T(8,128)}), f32[512,128]{0,1:T(8,128)}) %all-reduce.10.cloned.1.call-update) | async-done | bytes 262160 | tf_op jit(solution)/shard_map/psum | solution.py:101
  761.7 1.6 fusion.132
  763.3 1.0 fusion.136
  764.6 139.2 %all-reduce.14.cloned.1.call-done = f32[128,128]{1,0:T(8,128)} async-done(((f32[128,128]{1,0:T(8,128)}), f32[128,128]{1,0:T(8,128)}) %all-reduce.14.cloned.1.call-update) | async-done | bytes 65552 | tf_op jit(solution)/shard_map/psum | solution.py:103
  903.9 1.2 fusion.131
  905.1 1.3 fusion.48
  906.4 1.5 convolution_negate_fusion
  907.9 98.7 %all-gather.5.cloned.1.call-done = f32[16384,128]{1,0:T(8,128)} async-done(((f32[512,128]{1,0:T(8,128)}), f32[16384,128]{1,0:T(8,128)}) %all-gather.5.cloned.1.call-update) | async-done | bytes 8388624 | tf_op jit(solution)/shard_map/all_gather | solution.py:106
  1006.7 5.0 fusion.49
  1011.7 6.7 subtract_subtract_fusion
  (608 shorter events, 195.8 us)
Async XLA Ops:
  7.2 1.0 copy-start
  7.2 145.8 %all-reduce.6.cloned.1.call-start = ((), (), s32[]{:S(2)}) async-start(), calls=%async_computation | async-start | bytes 131072 | tf_op jit(solution)/shard_map/psum | solution.py:86
  9.4 309.4 %all-reduce.8.cloned.1.call-start = ((), (), s32[]{:S(2)}) async-start(), calls=%async_computation.1 | async-start | bytes 131072 | tf_op jit(solution)/shard_map/psum | solution.py:89
  167.8 738.6 %copy-start.4 = (f32[128,128]{1,0:T(8,128)}, f32[128,128]{1,0:T(8,128)S(1)}, u32[]{:S(2)}) copy-start(f32[128,128]{1,0:T(8,128)S(1)} %get-tuple-element.926) | copy-start | bytes 196612
  179.1 305.8 %all-reduce.12.cloned.1.call-start = ((), (), s32[]{:S(2)}) async-start(), calls=%async_computation.4 | async-start | bytes 131072 | tf_op jit(solution)/shard_map/psum | solution.py:11
  345.1 343.0 %all-gather.3.cloned.1.call-start = ((), (), s32[]{:S(2)}) async-start(), calls=%async_computation.2 | async-start | bytes 8650752 | tf_op jit(solution)/shard_map/all_gather | solution.py:98
  345.7 416.0 %all-reduce.10.cloned.1.call-start = ((), (), s32[]{:S(2)}) async-start(), calls=%async_computation.3 | async-start | bytes 524288 | tf_op jit(solution)/shard_map/psum | solution.py:101
  637.1 126.1 %copy-start.2 = (f32[512,128]{0,1:T(8,128)S(1)}, f32[512,128]{0,1:T(8,128)}, u32[]{:S(2)}) copy-start(f32[512,128]{0,1:T(8,128)} %get-tuple-element.927) | copy-start | bytes 786436
  695.7 208.2 %all-reduce.14.cloned.1.call-start = ((), (), s32[]{:S(2)}) async-start(), calls=%async_computation.5 | async-start | bytes 131072 | tf_op jit(solution)/shard_map/psum | solution.py:103
  764.3 242.3 %all-gather.5.cloned.1.call-start = ((), (), s32[]{:S(2)}) async-start(), calls=%async_computation.6 | async-start | bytes 8650752 | tf_op jit(solution)/shard_map/all_gather | solution.py:106
  906.4 105.3 %copy-start.3 = (f32[512,128]{1,0:T(8,128)S(1)}, f32[512,128]{1,0:T(8,128)}, u32[]{:S(2)}) copy-start(f32[512,128]{1,0:T(8,128)} %fusion.48) | copy-start | bytes 786436
  1006.7 5.1 copy-start.1
Sparse Core Ops, SparseCore 0:
  12.0 140.8 all-reduce.5
  179.2 139.5 all-reduce.7
  345.3 139.6 all-reduce.11
  487.9 100.0 all-gather.2
  695.8 65.7 all-reduce.9
  765.6 138.2 all-reduce.13
  907.0 99.5 all-gather.4
where the time goes:
time: 1030 us
  waiting for transfers between devices  726 us (70%)
  other arithmetic  166 us (16%)
  local copies, waits for them, and re-layouts  79.2 us (8%)
  matrix products  37.4 us (4%)
  between operations  14.5 us (1%)
    psum x1, waiting for transfers between devices, body(): first_gram = lax.psum(gram_of(panel_block), 'row')  144 us
    psum x1, waiting for transfers between devices, body(): second_gram = lax.psum(gram_of(first_basis), 'row')  139 us
    psum x1, waiting for transfers between devices, body(): inner_sum = lax.psum(gram_both(vectors, applied), 'row')  139 us
    psum x1, waiting for transfers between devices, broadcast(): return lax.psum(jnp.where(mine, shard, jnp.zeros_like(shard)), axis)  139 us
    div x128, other arithmetic, eliminate(): pivot_row = pivot_row / pivot_row[pivot]  106 us
    all_gather x1, waiting for transfers between devices, body(): all_update = lax.all_gather(row_update, 'row', axis=0, tiled=True)  98.7 us
    dynamic_slice x128, local copies, waits for them, and re-layouts, eliminate(): pivot_row = pivot_row / pivot_row[pivot]  74.9 us
    psum x1, waiting for transfers between devices, body(): row_product = lax.psum(partial_product, 'col')  65.7 us
  transfers between devices with their start and end apart: 7, of which 6 were waited for; matrix products, arithmetic and copies ran while one was open for 20% of the time, Pallas kernels for 0%

commit v1 on v0

v1 whole, which is shorter than its diff:
```python
import functools

import jax
import jax.numpy as jnp
from jax import lax
from jax.experimental import pallas as pl
from jax.experimental.pallas import tpu as pltpu
from jax.sharding import PartitionSpec as P

HIGH = lax.Precision.HIGHEST
F32 = jnp.float32
BF16 = jnp.bfloat16
MESH = pl.DeviceIdType.MESH
NX, NZ = 4, 8
NN = (((1,), (0,)), ((), ()))
NT = (((1,), (1,)), ((), ()))
TN = (((0,), (0,)), ((), ()))


def mm(a, b, dims=NN):
    return lax.dot_general(a, b, dims, precision=HIGH, preferred_element_type=F32)


def halves(a):
    top = a.astype(BF16)
    return top, (a - top.astype(F32)).astype(BF16)


def mm3(a, b, dims=NN):
    def one(p, q):
        return lax.dot_general(p, q, dims, preferred_element_type=F32)
    return one(a[0], b[0]) + (one(a[0], b[1]) + one(a[1], b[0]))


def eyes(shape, shift=0):
    return (lax.broadcasted_iota(jnp.int32, shape, 0) + shift) == lax.broadcasted_iota(jnp.int32, shape, 1)


def chol_inv(work, rows, bs):
    n = work.shape[0]
    for b in range(n // bs):
        lo = b * bs
        left = [work[lo + i:lo + i + 1, 0:n] for i in range(bs)]
        right = [work[lo + i:lo + i + 1, n:2 * n] for i in range(bs)]
        s = [[None] * bs for _ in range(bs)]
        for i in range(bs):
            for k in range(i + 1):
                s[i][k] = jnp.broadcast_to(left[i][:, lo + k:lo + k + 1], (1, n))
        scale = []
        for t in range(bs):
            inv = 1.0 / s[t][t]
            scale.append(lax.rsqrt(s[t][t]))
            fs = {i: s[i][t] * inv for i in range(t + 1, bs)}
            for i in range(t + 1, bs):
                for k in range(t + 1, i + 1):
                    s[i][k] = s[i][k] - (s[i][t] * s[k][t]) * inv
            for i in range(t + 1, bs):
                left[i] = left[i] - fs[i] * left[t]
                right[i] = right[i] - fs[i] * right[t]
        for i in range(bs):
            rows[lo + i:lo + i + 1, 0:n] = left[i] * scale[i]
            rows[lo + i:lo + i + 1, n:2 * n] = right[i] * scale[i]
        if lo + bs < n:
            blk = rows[lo:lo + bs, :]
            work[lo + bs:, :] = work[lo + bs:, :] - mm(blk[:, lo + bs:n], blk, TN)


def gj_inverse(work, bs):
    n = work.shape[0]
    for b in range(n // bs):
        lo = b * bs
        left = [work[lo + i:lo + i + 1, 0:n] for i in range(bs)]
        right = [work[lo + i:lo + i + 1, n:2 * n] for i in range(bs)]
        s = [[jnp.broadcast_to(left[i][:, lo + k:lo + k + 1], (1, n)) for k in range(bs)] for i in range(bs)]
        for t in range(bs):
            inv = 1.0 / s[t][t]
            for k in range(t + 1, bs):
                s[t][k] = s[t][k] * inv
            left[t] = left[t] * inv
            right[t] = right[t] * inv
            for i in range(bs):
                if i == t:
                    continue
                for k in range(t + 1, bs):
                    s[i][k] = s[i][k] - s[i][t] * s[t][k]
                left[i] = left[i] - s[i][t] * left[t]
                right[i] = right[i] - s[i][t] * right[t]
        lefts = jnp.concatenate(left, axis=0)
        rights = jnp.concatenate(right, axis=0)
        both = jnp.concatenate([lefts, rights], axis=1)
        cols = work[:, lo:lo + bs]
        rowi = lax.broadcasted_iota(jnp.int32, cols.shape, 0)
        cols = jnp.where((rowi >= lo) & (rowi < lo + bs), 0.0, cols)
        work[...] = work[...] - mm(cols, both)
        work[lo:lo + bs, :] = both


def place():
    row = lax.axis_index("row")
    return row // NZ, row % NZ, lax.axis_index("col")


def groups(ncol):
    x, z, c = place()
    gx = [(((x + d) % NX) * NZ + z, c) for d in range(NX)]
    gz = [(x * NZ + (z + d) % NZ, c) for d in range(NZ)]
    gc = [(x * NZ + z, (c + d) % ncol) for d in range(ncol)]
    return gx, gz, gc


def greet(ncol):
    sem = pltpu.get_barrier_semaphore()
    gx, gz, gc = groups(ncol)
    peers = gx[1:] + gz[1:] + gc[1:]
    for peer in peers:
        pl.semaphore_signal(sem, inc=1, device_id=peer, device_id_type=MESH)
    return sem, len(peers)


def send(src, dst, ss, rs, peer):
    copy = pltpu.make_async_remote_copy(
        src_ref=src, dst_ref=dst, send_sem=ss, recv_sem=rs, device_id=peer, device_id_type=MESH)
    copy.start()
    return copy


def slot_sum(buf, me, count):
    total = buf[me]
    for a in range(1, count):
        total = total + buf[(me + count - a) % count]
    return total


class Reduce:
    def __init__(self, out, xbuf, zbuf, sems, ncol):
        self.out, self.xbuf, self.zbuf, self.ncol = out, xbuf, zbuf, ncol
        self.xs, self.xr, self.zs, self.zr, self.cs, self.cr = sems
        self.gx, self.gz, self.gc = groups(ncol)
        self.x, self.z, self.c = place()
        self.sl = out.shape[0] // ncol
        self.open = []

    def part(self):
        return pl.ds(pl.multiple_of(self.c * self.sl, 8), self.sl)

    def start_x(self, src):
        self.xbuf[0] = src[self.part(), :]
        self.now = [send(self.xbuf.at[0], self.xbuf.at[d], self.xs.at[d], self.xr.at[d], self.gx[d]) for d in range(1, NX)]

    def start_z(self):
        for copy in self.now:
            copy.wait_recv()
        self.open += self.now
        self.zbuf[0] = slot_sum(self.xbuf, self.x, NX)
        self.now = [send(self.zbuf.at[0], self.zbuf.at[d], self.zs.at[d], self.zr.at[d], self.gz[d]) for d in range(1, NZ)]

    def start_c(self):
        for copy in self.now:
            copy.wait_recv()
        self.open += self.now
        self.out[self.part(), :] = slot_sum(self.zbuf, self.z, NZ)
        mine = self.out.at[self.part(), :]
        self.now = [send(mine, mine, self.cs.at[d], self.cr.at[d], self.gc[d]) for d in range(1, self.ncol)]

    def finish(self):
        for d, copy in enumerate(self.now, 1):
            rows = pl.ds(pl.multiple_of(((self.c + self.ncol - d) % self.ncol) * self.sl, 8), self.sl)
            theirs = self.out.at[rows, :]
            pltpu.make_async_remote_copy(
                src_ref=theirs, dst_ref=theirs, send_sem=self.cs.at[d], recv_sem=self.cr.at[d],
                device_id=self.gc[d], device_id_type=MESH).wait_recv()
        for copy in self.open + self.now:
            copy.wait_send()


def reduce_scratch(height, ncol):
    sl = height // ncol
    dma = pltpu.SemaphoreType.DMA
    return [pltpu.VMEM((NX, sl, 128), F32), pltpu.VMEM((NZ, sl, 128), F32),
            dma((NX,)), dma((NX,)), dma((NZ,)), dma((NZ,)), dma((ncol,)), dma((ncol,))]


VM = pl.BlockSpec(memory_space=pltpu.VMEM)
ANY = pl.BlockSpec(memory_space=pl.ANY)


def comm_params(cid):
    return pltpu.CompilerParams(collective_id=cid, has_side_effects=True, vmem_limit_bytes=60 << 20)


def first_kernel(ncol, p_ref, out_ref, src, xbuf, zbuf, *sems):
    sem, count = greet(ncol)
    p = p_ref[...]
    src[0:128, :] = mm(p, p, TN)
    lead = jnp.where(lax.axis_index("row") == 0, 1.0, 0.0)
    src[128:256, :] = p[0:128, :] * lead
    pl.semaphore_wait(sem, count)
    red = Reduce(out_ref, xbuf, zbuf, sems, ncol)
    red.start_x(src)
    red.start_z()
    red.start_c()
    red.finish()


def sum_kernel(ncol, a_ref, b_ref, out_ref, src, xbuf, zbuf, *sems):
    sem, count = greet(ncol)
    src[...] = mm(a_ref[...], b_ref[...], TN)
    pl.semaphore_wait(sem, count)
    red = Reduce(out_ref, xbuf, zbuf, sems, ncol)
    red.start_x(src)
    red.start_z()
    red.start_c()
    red.finish()


def chol_one(g_ref, l_ref, li_ref, xt_ref, work, rows):
    n = 128
    work[:, 0:n] = g_ref[0:n, :]
    work[:, n:] = jnp.where(eyes((n, n)), 1.0, 0.0)
    chol_inv(work, rows, 16)
    low = lax.broadcasted_iota(jnp.int32, (n, n), 0) >= lax.broadcasted_iota(jnp.int32, (n, n), 1)
    l_ref[...] = jnp.where(low, rows[:, 0:n].T, 0.0)
    inv = jnp.where(low, rows[:, n:], 0.0)
    li_ref[...] = inv
    xt_ref[...] = mm(g_ref[n:, :], inv, NT)


def second_kernel(ncol, p_ref, li_ref, p0, p1, p2, p3, a_ref,
                  g_ref, xr_ref, xc_ref, yw_ref,
                  src, xbuf, zbuf, xs, xr, zs, zr, cs, cr,
                  av, yp, ybuf, wbuf, asem, ys, yr, ws, wr, fs, fr):
    x, z, c = place()
    load = pltpu.make_async_copy(a_ref, av, asem)
    load.start()
    sem, count = greet(ncol)
    li = li_ref[...]
    first = mm(p_ref[...], li, NT)
    xr_ref[...] = first
    src[...] = mm(first, first, TN)
    pl.semaphore_wait(sem, count)
    red = Reduce(g_ref, xbuf, zbuf, (xs, xr, zs, zr, cs, cr), ncol)
    red.start_x(src)
    load.wait()
    sl = yp.shape[0] // ncol
    gc = red.gc

    def wsend(d):
        part = av.at[pl.ds(pl.multiple_of(d * sl, 8), sl), 0:128]
        return pltpu.make_async_remote_copy(
            src_ref=part, dst_ref=wbuf, send_sem=ws.at[d], recv_sem=wr,
            device_id=gc[d], device_id_type=MESH)

    parts = (p0, p1, p2, p3)

    def block(i):
        xi = mm(parts[i][...], li, NT)
        xc_ref[i] = xi
        width = xi.shape[0]
        at = pl.multiple_of(((x + i) % 4) * width, 128)
        return mm3(halves(av[:, pl.ds(at, width)]), halves(xi))

    acc = block(0)
    red.start_z()
    acc = acc + block(1)
    acc = acc + block(2)
    red.start_c()
    acc = acc + block(3)
    yp[...] = acc

    def mine(d):
        return pl.ds(pl.multiple_of(((c + d) % ncol) * sl, 8), sl)

    ybuf[0] = yp[mine(0), :]
    ysends = [send(yp.at[mine(d), :], ybuf.at[d], ys.at[d], yr.at[d], gc[d]) for d in range(1, ncol)]

    @pl.when(c == 0)
    def _():
        for d in range(1, ncol):
            wsend(d).start()
        wbuf[...] = av[0:sl, 0:128]

    red.finish()
    for copy in ysends:
        copy.wait_recv()

    @pl.when(c != 0)
    def _():
        wsend(1).wait_recv()

    yw_ref[mine(0), 0:128] = slot_sum(ybuf, c, ncol)
    yw_ref[mine(0), 128:256] = wbuf[...]
    own = yw_ref.at[mine(0), :]
    fsends = [send(own, own, fs.at[d], fr.at[d], gc[d]) for d in range(1, ncol)]
    for d in range(1, ncol):
        theirs = yw_ref.at[mine(ncol - d), :]
        pltpu.make_async_remote_copy(
            src_ref=theirs, dst_ref=theirs, send_sem=fs.at[d], recv_sem=fr.at[d],
            device_id=gc[d], device_id_type=MESH).wait_recv()
    for copy in ysends + fsends:
        copy.wait_send()

    @pl.when(c == 0)
    def _():
        for d in range(1, ncol):
            wsend(d).wait_send()


def chol_two(g_ref, l1_ref, xt_ref, xr_ref, yw_ref, rowi_ref, band_ref, l2i_ref, m_ref, v_ref, av_ref, work, rows):
    n = 128
    work[:, 0:n] = g_ref[...]
    work[:, n:] = jnp.where(eyes((n, n)), 1.0, 0.0)
    chol_inv(work, rows, 16)
    low = lax.broadcasted_iota(jnp.int32, (n, n), 0) >= lax.broadcasted_iota(jnp.int32, (n, n), 1)
    inv = jnp.where(low, rows[:, n:], 0.0)
    upper = jnp.where(low, rows[:, 0:n].T, 0.0).T
    av_ref[...] = mm(yw_ref[:, 0:n], inv, NT) + yw_ref[:, n:]
    ident = jnp.where(eyes(v_ref.shape, rowi_ref[0] * v_ref.shape[0]), 1.0, 0.0)
    v_ref[...] = mm(xr_ref[...], inv, NT) + ident
    l2i_ref[...] = inv
    band_ref[...] = -mm(upper, l1_ref[...], NT)
    top = mm(xt_ref[...], inv, NT)
    m_ref[...] = top.T + jnp.where(eyes((n, n)), 1.0, 0.0)


def inverse_kernel(m_ref, k_ref, work):
    n = 128
    work[:, 0:n] = m_ref[...]
    work[:, n:] = jnp.where(eyes((n, n)), 1.0, 0.0)
    gj_inverse(work, 8)
    k_ref[...] = work[:, n:]


def last_kernel(place_ref, k_ref, s_ref, l2i_ref, v_ref, avr_ref, xc_ref, q0, q1, q2, q3, a_ref, out_ref,
                abuf, obuf, vc, insem, outsem):
    n = 128
    width = q0.shape[0]

    def cols(i):
        return pl.ds(pl.multiple_of(((place_ref[0] + i) % 4) * width, 128), width)

    loads = [pltpu.make_async_copy(a_ref.at[:, cols(i)], abuf.at[i], insem.at[i]) for i in range(4)]
    for copy in loads:
        copy.start()
    k = k_ref[...]
    inner = mm(k, mm(s_ref[...], k), TN)
    both = -0.5 * (inner + inner.T)
    right = jnp.concatenate([
        jnp.concatenate([jnp.zeros((n, n), F32), k], axis=1),
        jnp.concatenate([k.T, both], axis=1)], axis=0)
    pair = jnp.concatenate([avr_ref[...], v_ref[...]], axis=1)
    lead = halves(mm(pair, right))
    stores = []
    for i, q in enumerate((q0, q1, q2, q3)):
        shift = (place_ref[1] * 4 + (place_ref[0] + i) % 4) * width
        vi = mm(xc_ref[i], l2i_ref[...], NT) + jnp.where(eyes((width, n), shift), 1.0, 0.0)
        tail = halves(jnp.concatenate([q[...], vi], axis=1))
        prod = mm3(lead, tail, NT)
        loads[i].wait()
        obuf[i] = abuf[i] - prod
        copy = pltpu.make_async_copy(obuf.at[i], out_ref.at[:, cols(i)], outsem.at[i])
        copy.start()
        stores.append(copy)
    for copy in stores:
        copy.wait()


def struct(*shape):
    return jax.ShapeDtypeStruct(shape, F32)


def spread(block, nrow, ncol):
    out = []
    for i in range(4):
        perm = []
        for xq in range(NX):
            for zq in range(NZ):
                for cq in range(ncol):
                    core, k = zq // 4, zq % 4
                    xd = (k - i) % 4
                    perm.append(((xq * NZ + zq) * ncol + cq, (xd * NZ + cq) * ncol + xq * 2 + core))
        out.append(lax.ppermute(block, ("row", "col"), perm))
    return out


def body(nrow, ncol, panel, trailing):
    n = panel.shape[1]
    height, width = trailing.shape
    row = lax.axis_index("row")
    col = lax.axis_index("col")
    pc = spread(panel, nrow, ncol)

    gt = pl.pallas_call(
        functools.partial(first_kernel, ncol), out_shape=struct(2 * n, n), in_specs=[VM], out_specs=VM,
        scratch_shapes=[pltpu.VMEM((2 * n, n), F32)] + reduce_scratch(2 * n, ncol),
        compiler_params=comm_params(0))(panel)

    wide = pltpu.VMEM((n, 2 * n), F32)
    l1, l1i, xt = pl.pallas_call(
        chol_one, out_shape=(struct(n, n),) * 3, in_specs=[VM], out_specs=(VM,) * 3,
        scratch_shapes=[wide, wide])(gt)

    dma = pltpu.SemaphoreType.DMA
    sl = height // ncol
    g2, xr, xc, yw = pl.pallas_call(
        functools.partial(second_kernel, ncol),
        out_shape=(struct(n, n), struct(height, n), struct(4, height, n), struct(height, 2 * n)),
        in_specs=[VM] * 6 + [ANY], out_specs=(VM,) * 4,
        scratch_shapes=[pltpu.VMEM((n, n), F32)] + reduce_scratch(n, ncol) + [
            pltpu.VMEM((height, width), F32), pltpu.VMEM((height, n), F32),
            pltpu.VMEM((ncol, sl, n), F32), pltpu.VMEM((sl, n), F32), dma,
            dma((ncol,)), dma((ncol,)), dma((ncol,)), dma, dma((ncol,)), dma((ncol,))],
        compiler_params=comm_params(1))(panel, l1i, *pc, trailing)

    SM = pl.BlockSpec(memory_space=pltpu.SMEM)
    band, l2i, m, v, av = pl.pallas_call(
        chol_two, out_shape=(struct(n, n), struct(n, n), struct(n, n), struct(height, n), struct(height, n)),
        in_specs=[VM] * 5 + [SM], out_specs=(VM,) * 5,
        scratch_shapes=[wide, wide])(g2, l1, xt, xr, yw, row[None])

    qc = spread(av, nrow, ncol)
    s = pl.pallas_call(
        functools.partial(sum_kernel, ncol), out_shape=struct(n, n), in_specs=[VM] * 2, out_specs=VM,
        scratch_shapes=[pltpu.VMEM((n, n), F32)] + reduce_scratch(n, ncol),
        compiler_params=comm_params(2))(v, av)
    k = pl.pallas_call(
        inverse_kernel, out_shape=struct(n, n), in_specs=[VM], out_specs=VM, scratch_shapes=[wide])(m)

    where = jnp.stack([row // NZ, col])
    reduced = pl.pallas_call(
        last_kernel, out_shape=struct(height, width),
        in_specs=[SM] + [VM] * 10 + [ANY], out_specs=ANY,
        scratch_shapes=[pltpu.VMEM((4, height, width // 4), F32)] * 2 + [
            pltpu.VMEM((height, n), F32), dma((4,)), dma((4,))],
        compiler_params=pltpu.CompilerParams(vmem_limit_bytes=60 << 20),
    )(where, k, s, l2i, v, av, xc, *qc, trailing)
    return reduced, band, l1


def solution(mesh):
    nrow, ncol = mesh.shape["row"], mesh.shape["col"]
    return jax.shard_map(
        functools.partial(body, nrow, ncol), mesh=mesh, in_specs=(P("row", None), P("row", "col")),
        out_specs=(P("row", "col"), P(), P()), check_vma=False)
```

time: 1030 us -> 241 us (0.23)
  waiting for transfers between devices: 726 us -> 0.02 us
  Pallas kernels: 0 us -> 208 us
  other arithmetic: 166 us -> 0.66 us
  local copies, waits for them, and re-layouts: 79.2 us -> 1.86 us
  matrix products: 37.4 us -> 0 us
  starting transfers between devices: 0.95 us -> 28.8 us
  between operations: 14.5 us -> 1.02 us
    psum x5 -> x0, waiting for transfers between devices: 627 us -> none  [the longest x1 144 us: body(): first_gram = lax.psum(gram_of(panel_block), 'row')]
    pallas_call x0 -> x7, Pallas kernels: none -> 208 us  [the longest x1 73 us: body(): pl.pallas_call(functools.partial(first_kernel, ncol), out_shape=struct(2...]
    div x130 -> x0, other arithmetic: 107 us -> none  [the longest x128 106 us: eliminate(): pivot_row = pivot_row / pivot_row[pivot]]
    all_gather x2 -> x0, waiting for transfers between devices: 98.8 us -> none  [the longest x1 98.7 us: body(): all_update = lax.all_gather(row_update, 'row', axis=0, tiled=True)]
    dynamic_slice x128 -> x0, local copies, waits for them, and re-layouts: 74.9 us -> none  [eliminate(): pivot_row = pivot_row / pivot_row[pivot]]
    another operation x10 -> x1, other arithmetic: 45.6 us -> 0.66 us  [body(): where = jnp.stack([row // NZ, col])]
    dot_general x52 -> x0, matrix products: 35.8 us -> none  [the longest x47 20.8 us: times_of(): jnp.dot(left, right, precision=HIGH, preferred_element_type=jnp.float32)]
    ppermute x0 -> x8, starting transfers between devices: none -> 28.8 us  [spread(): out.append(lax.ppermute(block, ('row', 'col'), perm))]
  transfers between devices with their start and end apart: 7 -> 8, of which waited for: 6 -> 0; matrix products, arithmetic and copies ran while one was open for 20% -> 0% of each run, Pallas kernels for 0% -> 63%
where the time goes in v1:
time: 241 us; the launch traced here: 240 us
  Pallas kernels  208 us (86%)
  starting transfers between devices  28.8 us (12%)
    pallas_call x1, Pallas kernels, body(): pl.pallas_call(functools.partial(first_kernel, ncol), out_shape=struct(2...  73 us
    pallas_call x1, Pallas kernels, body(): pl.pallas_call(functools.partial(sum_kernel, ncol), out_shape=struct(n, n...  61.6 us
    pallas_call x1, Pallas kernels, body(): pl.pallas_call(functools.partial(second_kernel, ncol), out_shape=(struct(...  37.3 us
    ppermute x8, starting transfers between devices, spread(): out.append(lax.ppermute(block, ('row', 'col'), perm))  28.8 us
    pallas_call x1, Pallas kernels, body(): pl.pallas_call(inverse_kernel, out_shape=struct(n, n), in_specs=[VM], out...  9.52 us
    pallas_call x1, Pallas kernels, body(): pl.pallas_call(last_kernel, out_shape=struct(height, width), in_specs=[SM...  9.24 us
    pallas_call x1, Pallas kernels, body(): pl.pallas_call(chol_two, out_shape=(struct(n, n), struct(n, n), struct(n,...  8.99 us
    pallas_call x1, Pallas kernels, body(): pl.pallas_call(chol_one, out_shape=(struct(n, n),) * 3, in_specs=[VM], ou...  8.04 us
  transfers between devices with their start and end apart: 8, of which 0 were waited for; matrix products, arithmetic and copies ran while one was open for 0% of the time, Pallas kernels for 63%

profile of v1, /device:TPU:1, one launch (start us, length us, event | category | flops | bytes accessed | tf_op | source)
XLA Modules:
  0.0 240.0 jit_solution(12826186456988312634)
XLA Ops:
  0.6 5.6 %collective-permute-start.2 = (f32[512,128]{1,0:T(8,128)}, f32[512,128]{1,0:T(8,128)S(1)}, u32[]{:S(2)}, u32[]{:S(2)}) collective-permute-start(f32[512,128]{1,0:T(8,128)} %p_ref.3), channel_id=1, source_target_pairs={{0,128},{1,136},{2,144},{3,152},{4,160},{5,168},{6,176},{7,184},{8... | collective-permute-start | bytes 786440 | tf_op jit(solution)/shard_map/ppermute | solution.py:381
  6.2 4.2 %collective-permute-start.1 = (f32[512,128]{1,0:T(8,128)}, f32[512,128]{1,0:T(8,128)S(1)}, u32[]{:S(2)}, u32[]{:S(2)}) collective-permute-start(f32[512,128]{1,0:T(8,128)} %p_ref.3), channel_id=1, source_target_pairs={{0,192},{1,200},{2,208},{3,216},{4,224},{5,232},{6,240},{7,248},{8... | collective-permute-start | bytes 786440 | tf_op jit(solution)/shard_map/ppermute | solution.py:381
  10.4 1.9 collective-permute-start
  12.3 6.2 %collective-permute-start.3 = (f32[512,128]{1,0:T(8,128)}, f32[512,128]{1,0:T(8,128)S(1)}, u32[]{:S(2)}, u32[]{:S(2)}) collective-permute-start(f32[512,128]{1,0:T(8,128)} %p_ref.3), channel_id=1, source_target_pairs={{0,64},{1,72},{2,80},{3,88},{4,96},{5,104},{6,112},{7,120},{8,128}... | collective-permute-start | bytes 786440 | tf_op jit(solution)/shard_map/ppermute | solution.py:381
  18.6 73.0 %shard_map.49.g_ref = f32[256,128]{1,0:T(8,128)} custom-call(f32[512,128]{1,0:T(8,128)} %p_ref.3), custom_call_target="tpu_custom_call" | custom-call | tf_op jit(solution)/shard_map/pallas_call | solution.py:392
  91.6 8.0 %shard_map.50 = (f32[128,128]{1,0:T(8,128)}, f32[128,128]{1,0:T(8,128)}, f32[128,128]{1,0:T(8,128)}) custom-call(f32[256,128]{1,0:T(8,128)} %shard_map.49.g_ref), custom_call_target="tpu_custom_call" | custom-call | tf_op jit(solution)/shard_map/pallas_call | solution.py:398
  99.6 0.0 collective-permute-done.2.p2
  99.6 0.0 copy-start.4
  99.6 0.0 collective-permute-done.1.p1
  99.6 0.0 copy-start.5
  99.6 0.0 collective-permute-done.p0
  99.6 0.0 copy-start.6
  99.6 0.0 collective-permute-done.3.p3
  99.6 0.0 copy-start.7
  99.7 0.7 copy-done.4
  100.3 0.1 copy-done.5
  100.4 0.1 copy-done.6
  100.5 0.1 copy-done.7
  100.6 37.3 %shard_map.51 = (f32[128,128]{1,0:T(8,128)}, f32[512,128]{1,0:T(8,128)}, f32[4,512,128]{2,1,0:T(8,128)}, f32[512,256]{1,0:T(8,128)}) custom-call(f32[512,128]{1,0:T(8,128)} %p_ref.3, f32[128,128]{1,0:T(8,128)} %get-tuple-element.15.li_ref, f32[512,128]{1,0:T(8,128)} %copy-done.6, f32[512,128]{1,0:T(8,128)} %copy-done.5, f32[512,128]{1,0:T(8,128)} %copy-done.4, ...), custom_call_target="tpu_custom_call" | custom-call | tf_op jit(solution)/shard_map/pallas_call | solution.py:404
  137.8 9.0 %shard_map.52 = (f32[128,128]{1,0:T(8,128)}, f32[128,128]{1,0:T(8,128)}, f32[128,128]{1,0:T(8,128)}, f32[512,128]{1,0:T(8,128)}, f32[512,128]{1,0:T(8,128)}) custom-call(f32[128,128]{1,0:T(8,128)} %get-tuple-element.16.g_ref, f32[128,128]{1,0:T(8,128)} %get-tuple-element.14.l1_ref, f32[128,128]{1,0:T(8,128)} %get-tuple-element.18.xt_ref, ...), custom_call_target="tpu_custom_call" | custom-call | tf_op jit(solution)/shard_map/pallas_call | solution.py:415
  146.8 3.5 %collective-permute-start.7 = (f32[512,128]{1,0:T(8,128)}, f32[512,128]{1,0:T(8,128)S(1)}, u32[]{:S(2)}, u32[]{:S(2)}) collective-permute-start(f32[512,128]{1,0:T(8,128)} %get-tuple-element.23.b_ref.avr_ref), channel_id=1, source_target_pairs={{0,64},{1,72},{2,80},{3,88},{4,96},{5,104},{6,112},{7,120},{8,128}... | collective-permute-start | bytes 786440 | tf_op jit(solution)/shard_map/ppermute | solution.py:381
  150.3 0.9 collective-permute-start.6
  151.1 4.5 %collective-permute-start.5 = (f32[512,128]{1,0:T(8,128)}, f32[512,128]{1,0:T(8,128)S(1)}, u32[]{:S(2)}, u32[]{:S(2)}) collective-permute-start(f32[512,128]{1,0:T(8,128)} %get-tuple-element.23.b_ref.avr_ref), channel_id=1, source_target_pairs={{0,192},{1,200},{2,208},{3,216},{4,224},{5,232},{6,240},{7,248},{8... | collective-permute-start | bytes 786440 | tf_op jit(solution)/shard_map/ppermute | solution.py:381
  155.6 2.1 collective-permute-start.4
  157.8 0.7 pad_add_fusion.place_ref
  158.4 9.5 %shard_map.53.k_ref = f32[128,128]{1,0:T(8,128)} custom-call(f32[128,128]{1,0:T(8,128)} %get-tuple-element.21.m_ref), custom_call_target="tpu_custom_call" | custom-call | tf_op jit(solution)/shard_map/pallas_call | solution.py:425
  168.0 61.6 %shard_map.54.s_ref = f32[128,128]{1,0:T(8,128)} custom-call(f32[512,128]{1,0:T(8,128)} %get-tuple-element.22.a_ref.v_ref, f32[512,128]{1,0:T(8,128)} %get-tuple-element.23.b_ref.avr_ref), custom_call_target="tpu_custom_call" | custom-call | tf_op jit(solution)/shard_map/pallas_call | solution.py:421
  229.6 0.0 collective-permute-done.7.q3
  229.6 0.0 copy-start
  229.6 0.0 collective-permute-done.6.q2
  229.6 0.0 copy-start.1
  229.6 0.0 collective-permute-done.5.q1
  229.6 0.0 copy-start.2
  229.7 0.0 collective-permute-done.4.q0
  229.7 0.0 copy-start.3
  229.7 0.6 copy-done
  230.3 0.1 copy-done.1
  230.4 0.1 copy-done.2
  230.5 0.1 copy-done.3
  230.6 9.2 %shard_map.55 = f32[512,2048]{1,0:T(8,128)} custom-call(s32[2]{0:T(128)} %pad_add_fusion.place_ref, f32[128,128]{1,0:T(8,128)} %shard_map.53.k_ref, f32[128,128]{1,0:T(8,128)} %shard_map.54.s_ref, f32[128,128]{1,0:T(8,128)} %get-tuple-element.24.l2i_ref, f32[512,128]{1,0:T(8,128)} %get-tuple-element.22.a_ref.v_ref, ...), custom_call_target="tpu_custom_call" | custom-call | tf_op jit(solution)/shard_map/pallas_call | solution.py:429
Async XLA Ops:
  0.6 99.0 %collective-permute-start.2 = (f32[512,128]{1,0:T(8,128)}, f32[512,128]{1,0:T(8,128)S(1)}, u32[]{:S(2)}, u32[]{:S(2)}) collective-permute-start(f32[512,128]{1,0:T(8,128)} %p_ref.3), channel_id=1, source_target_pairs={{0,128},{1,136},{2,144},{3,152},{4,160},{5,168},{6,176},{7,184},{8... | collective-permute-start | bytes 786440 | tf_op jit(solution)/shard_map/ppermute | solution.py:381
  6.2 93.4 %collective-permute-start.1 = (f32[512,128]{1,0:T(8,128)}, f32[512,128]{1,0:T(8,128)S(1)}, u32[]{:S(2)}, u32[]{:S(2)}) collective-permute-start(f32[512,128]{1,0:T(8,128)} %p_ref.3), channel_id=1, source_target_pairs={{0,192},{1,200},{2,208},{3,216},{4,224},{5,232},{6,240},{7,248},{8... | collective-permute-start | bytes 786440 | tf_op jit(solution)/shard_map/ppermute | solution.py:381
  10.4 89.2 %collective-permute-start = (f32[512,128]{1,0:T(8,128)}, f32[512,128]{1,0:T(8,128)S(1)}, u32[]{:S(2)}, u32[]{:S(2)}) collective-permute-start(f32[512,128]{1,0:T(8,128)} %p_ref.3), channel_id=1, source_target_pairs={{0,0},{1,8},{2,16},{3,24},{4,32},{5,40},{6,48},{7,56},{8,64},{9,72... | collective-permute-start | bytes 786440 | tf_op jit(solution)/shard_map/ppermute | solution.py:381
  12.3 87.3 %collective-permute-start.3 = (f32[512,128]{1,0:T(8,128)}, f32[512,128]{1,0:T(8,128)S(1)}, u32[]{:S(2)}, u32[]{:S(2)}) collective-permute-start(f32[512,128]{1,0:T(8,128)} %p_ref.3), channel_id=1, source_target_pairs={{0,64},{1,72},{2,80},{3,88},{4,96},{5,104},{6,112},{7,120},{8,128}... | collective-permute-start | bytes 786440 | tf_op jit(solution)/shard_map/ppermute | solution.py:381
  99.6 0.7 copy-start.4
  99.6 0.8 copy-start.5
  99.6 0.8 copy-start.6
  99.6 0.9 copy-start.7
  146.8 82.8 %collective-permute-start.7 = (f32[512,128]{1,0:T(8,128)}, f32[512,128]{1,0:T(8,128)S(1)}, u32[]{:S(2)}, u32[]{:S(2)}) collective-permute-start(f32[512,128]{1,0:T(8,128)} %get-tuple-element.23.b_ref.avr_ref), channel_id=1, source_target_pairs={{0,64},{1,72},{2,80},{3,88},{4,96},{5,104},{6,112},{7,120},{8,128}... | collective-permute-start | bytes 786440 | tf_op jit(solution)/shard_map/ppermute | solution.py:381
  150.3 79.3 %collective-permute-start.6 = (f32[512,128]{1,0:T(8,128)}, f32[512,128]{1,0:T(8,128)S(1)}, u32[]{:S(2)}, u32[]{:S(2)}) collective-permute-start(f32[512,128]{1,0:T(8,128)} %get-tuple-element.23.b_ref.avr_ref), channel_id=1, source_target_pairs={{0,128},{1,136},{2,144},{3,152},{4,160},{5,168},{6,176},{7,184},{8... | collective-permute-start | bytes 786440 | tf_op jit(solution)/shard_map/ppermute | solution.py:381
  151.1 78.5 %collective-permute-start.5 = (f32[512,128]{1,0:T(8,128)}, f32[512,128]{1,0:T(8,128)S(1)}, u32[]{:S(2)}, u32[]{:S(2)}) collective-permute-start(f32[512,128]{1,0:T(8,128)} %get-tuple-element.23.b_ref.avr_ref), channel_id=1, source_target_pairs={{0,192},{1,200},{2,208},{3,216},{4,224},{5,232},{6,240},{7,248},{8... | collective-permute-start | bytes 786440 | tf_op jit(solution)/shard_map/ppermute | solution.py:381
  155.6 74.0 %collective-permute-start.4 = (f32[512,128]{1,0:T(8,128)}, f32[512,128]{1,0:T(8,128)S(1)}, u32[]{:S(2)}, u32[]{:S(2)}) collective-permute-start(f32[512,128]{1,0:T(8,128)} %get-tuple-element.23.b_ref.avr_ref), channel_id=1, source_target_pairs={{0,0},{1,8},{2,16},{3,24},{4,32},{5,40},{6,48},{7,56},{8,64},{9,72... | collective-permute-start | bytes 786440 | tf_op jit(solution)/shard_map/ppermute | solution.py:381
  229.6 0.7 copy-start
  229.6 0.8 copy-start.1
  229.6 0.8 copy-start.2
  229.7 0.9 copy-start.3

commit v2 on v0

v2 whole, which is shorter than its diff:
```python
import functools

import jax
import jax.numpy as jnp
from jax import lax
from jax.experimental import pallas as pl
from jax.experimental.pallas import tpu as pltpu
from jax.sharding import PartitionSpec as P

HIGH = lax.Precision.HIGHEST
F32 = jnp.float32
BF16 = jnp.bfloat16
MESH = pl.DeviceIdType.MESH
NX, NZ = 4, 8
BS = 16
NN = (((1,), (0,)), ((), ()))
NT = (((1,), (1,)), ((), ()))
TN = (((0,), (0,)), ((), ()))


def mm(a, b, dims=NN):
    return lax.dot_general(a, b, dims, precision=HIGH, preferred_element_type=F32)


def halves(a):
    top = a.astype(BF16)
    return top, (a - top.astype(F32)).astype(BF16)


def mm3(a, b, dims=NN):
    def one(p, q):
        return lax.dot_general(p, q, dims, preferred_element_type=F32)
    return one(a[0], b[0]) + (one(a[0], b[1]) + one(a[1], b[0]))


def eyes(shape, shift=0):
    return (lax.broadcasted_iota(jnp.int32, shape, 0) + shift) == lax.broadcasted_iota(jnp.int32, shape, 1)


def over(row, count):
    return jnp.broadcast_to(row, (count, row.shape[1]))


def eliminate(work, lo, hot, jordan):
    n = work.shape[0]
    bs = len(hot)
    rows = work[lo:lo + bs, :]
    col = [jnp.broadcast_to(rows[:, lo + k:lo + k + 1], (bs, n)) for k in range(bs)]
    pivots = []
    left, right = rows[:, 0:n], rows[:, n:]
    for t in range(bs):
        pivot = over(col[t][t:t + 1, :], bs)
        pivots.append(pivot[0:1, :])
        inv = 1.0 / pivot
        f = col[t] - hot[t] if jordan else jnp.where(hot[t], col[t], 0.0)
        for k in range(t + 1, bs):
            col[k] = col[k] - (f * over(col[k][t:t + 1, :], bs)) * inv
        g = f * inv
        left = left - g * over(left[t:t + 1, :], bs)
        right = right - g * over(right[t:t + 1, :], bs)
    return left, right, pivots


def chol_inv(work, rows, hooks=()):
    n = work.shape[0]
    at = lax.broadcasted_iota(jnp.int32, (BS, n), 0)
    hot = [at > t for t in range(BS)]
    for b in range(n // BS):
        lo = b * BS
        left, right, pivots = eliminate(work, lo, hot, False)
        scale = lax.rsqrt(jnp.concatenate(pivots, axis=0))
        blk = jnp.concatenate([left * scale, right * scale], axis=1)
        rows[lo:lo + BS, :] = blk
        if lo + BS < n:
            work[lo + BS:, :] = work[lo + BS:, :] - mm(blk[:, lo + BS:n], blk, TN)
        if b in hooks:
            hooks[b]()


def gj_inverse(work, hooks=()):
    n = work.shape[0]
    at = lax.broadcasted_iota(jnp.int32, (BS, n), 0)
    hot = [jnp.where(at == t, 1.0, 0.0) for t in range(BS)]
    for b in range(n // BS):
        lo = b * BS
        left, right, _ = eliminate(work, lo, hot, True)
        both = jnp.concatenate([left, right], axis=1)
        cols = work[:, lo:lo + BS]
        rowi = lax.broadcasted_iota(jnp.int32, cols.shape, 0)
        cols = jnp.where((rowi >= lo) & (rowi < lo + BS), 0.0, cols)
        work[...] = work[...] - mm(cols, both)
        work[lo:lo + BS, :] = both
        if b in hooks:
            hooks[b]()


def with_identity(work, square):
    n = work.shape[0]
    work[:, 0:n] = square
    work[:, n:] = jnp.where(eyes((n, n)), 1.0, 0.0)


def factors(rows):
    n = rows.shape[0]
    low = lax.broadcasted_iota(jnp.int32, (n, n), 0) >= lax.broadcasted_iota(jnp.int32, (n, n), 1)
    return jnp.where(low, rows[:, 0:n].T, 0.0), jnp.where(low, rows[:, n:], 0.0)


def place():
    row = lax.axis_index("row")
    return row // NZ, row % NZ, lax.axis_index("col")


def groups(ncol):
    x, z, c = place()
    gx = [(((x + d) % NX) * NZ + z, c) for d in range(NX)]
    gz = [(x * NZ + (z + d) % NZ, c) for d in range(NZ)]
    gc = [(x * NZ + z, (c + d) % ncol) for d in range(ncol)]
    return gx, gz, gc


def greet(ncol):
    sem = pltpu.get_barrier_semaphore()
    gx, gz, gc = groups(ncol)
    peers = gx[1:] + gz[1:] + gc[1:]
    for peer in peers:
        pl.semaphore_signal(sem, inc=1, device_id=peer, device_id_type=MESH)
    return sem, len(peers)


def send(src, dst, ss, rs, peer):
    copy = pltpu.make_async_remote_copy(
        src_ref=src, dst_ref=dst, send_sem=ss, recv_sem=rs, device_id=peer, device_id_type=MESH)
    copy.start()
    return copy


def slot_sum(buf, me, count):
    total = buf[me]
    for a in range(1, count):
        total = total + buf[(me + count - a) % count]
    return total


class Reduce:
    def __init__(self, out, xbuf, zbuf, sems, ncol):
        self.out, self.xbuf, self.zbuf, self.ncol = out, xbuf, zbuf, ncol
        self.xs, self.xr, self.zs, self.zr, self.cs, self.cr = sems
        self.gx, self.gz, self.gc = groups(ncol)
        self.x, self.z, self.c = place()
        self.sl = out.shape[0] // ncol
        self.open = []

    def part(self):
        return pl.ds(pl.multiple_of(self.c * self.sl, 8), self.sl)

    def start_x(self, src):
        self.xbuf[0] = src[self.part(), :]
        self.now = [send(self.xbuf.at[0], self.xbuf.at[d], self.xs.at[d], self.xr.at[d], self.gx[d]) for d in range(1, NX)]

    def start_z(self):
        for copy in self.now:
            copy.wait_recv()
        self.open += self.now
        self.zbuf[0] = slot_sum(self.xbuf, self.x, NX)
        self.now = [send(self.zbuf.at[0], self.zbuf.at[d], self.zs.at[d], self.zr.at[d], self.gz[d]) for d in range(1, NZ)]

    def start_c(self):
        for copy in self.now:
            copy.wait_recv()
        self.open += self.now
        self.out[self.part(), :] = slot_sum(self.zbuf, self.z, NZ)
        mine = self.out.at[self.part(), :]
        self.now = [send(mine, mine, self.cs.at[d], self.cr.at[d], self.gc[d]) for d in range(1, self.ncol)]

    def finish(self):
        for d, copy in enumerate(self.now, 1):
            rows = pl.ds(pl.multiple_of(((self.c + self.ncol - d) % self.ncol) * self.sl, 8), self.sl)
            theirs = self.out.at[rows, :]
            pltpu.make_async_remote_copy(
                src_ref=theirs, dst_ref=theirs, send_sem=self.cs.at[d], recv_sem=self.cr.at[d],
                device_id=self.gc[d], device_id_type=MESH).wait_recv()
        for copy in self.open + self.now:
            copy.wait_send()


def reduce_scratch(height, ncol):
    sl = height // ncol
    dma = pltpu.SemaphoreType.DMA
    return [pltpu.VMEM((NX, sl, 128), F32), pltpu.VMEM((NZ, sl, 128), F32),
            dma((NX,)), dma((NX,)), dma((NZ,)), dma((NZ,)), dma((ncol,)), dma((ncol,))]


VM = pl.BlockSpec(memory_space=pltpu.VMEM)
ANY = pl.BlockSpec(memory_space=pl.ANY)


def comm_params(cid):
    return pltpu.CompilerParams(collective_id=cid, has_side_effects=True, vmem_limit_bytes=60 << 20)


def turn(y):
    return (y + 2) % 3 + y // 3


def unturn(t):
    return (t + 1) % 3 * (1 - t // 3) + 3 * (t // 3)


class Gather:
    def __init__(self, src, out, sems, ncol):
        self.src, self.out = src, out
        self.s1, self.r1, self.s2, self.r2 = sems
        self.x, self.z, self.c = place()
        y, core = self.c // 2, self.c % 2
        self.quarter = src.shape[0] // NX
        xd = (turn(y) + NX - self.x) % NX
        self.xd = xd
        self.to = [((xd * NZ) + 2 * j + core, self.x * 2 + self.z // 4) for j in range(4)]
        ys = unturn((self.x + y) % NX)
        self.frm = [(y * NZ + 4 * core + k, ys * 2 + self.z % 2) for k in range(4)]
        self.gx = groups(ncol)[0]

    def rows(self, x):
        return pl.ds(pl.multiple_of(x * self.quarter, 128), self.quarter)

    def start_one(self):
        k = self.z % 4
        self.one = [send(self.src.at[self.rows(self.xd), :], self.out.at[k, self.rows(self.xd), :],
                         self.s1.at[j], self.r1.at[k], self.to[j]) for j in range(4)]

    def start_two(self):
        self.two = []
        for j in range(4):
            k = (self.z + j) % 4
            part = self.out.at[k, self.rows(self.x), :]
            pltpu.make_async_remote_copy(
                src_ref=part, dst_ref=part, send_sem=self.s1.at[j], recv_sem=self.r1.at[k],
                device_id=self.frm[0], device_id_type=MESH).wait_recv()
            self.two += [send(part, part, self.s2.at[d, j], self.r2.at[d, k], self.gx[d]) for d in range(1, NX)]

    def block(self, k):
        for d in range(1, NX):
            part = self.out.at[k, self.rows((self.x + NX - d) % NX), :]
            pltpu.make_async_remote_copy(
                src_ref=part, dst_ref=part, send_sem=self.s2.at[d, k], recv_sem=self.r2.at[d, k],
                device_id=self.gx[d], device_id_type=MESH).wait_recv()

    def finish(self):
        for copy in self.one + self.two:
            copy.wait_send()


def gather_sems():
    dma = pltpu.SemaphoreType.DMA
    return [dma((4,)), dma((4,)), dma((NX, 4)), dma((NX, 4))]


VM = pl.BlockSpec(memory_space=pltpu.VMEM)
ANY = pl.BlockSpec(memory_space=pl.ANY)


def struct(*shape):
    return jax.ShapeDtypeStruct(shape, F32)


def main_kernel(ncol, p_ref, a_ref, l1_ref, band_ref, lead_ref, avc_ref, vc_ref, *scratch):
    scratch = list(scratch)

    def take(count):
        head = scratch[:count]
        del scratch[:count]
        return head

    src1, out1, src2, out2, src3, out3 = take(6)
    red1, red2, red3 = take(8), take(8), take(8)
    gs1, gs2 = take(4), take(4)
    av, pc, work, rows, yp, ybuf, wbuf, yw, avr = take(9)
    asem, ys, yr, ws, wr, fs, fr = take(7)
    n = p_ref.shape[1]
    height = p_ref.shape[0]
    row, c = lax.axis_index("row"), lax.axis_index("col")

    load = pltpu.make_async_copy(a_ref, av, asem)
    load.start()
    sem, count = greet(ncol)
    early = Gather(p_ref, pc, gs1, ncol)
    late = Gather(avr, avc_ref, gs2, ncol)
    for peer in early.to + early.frm:
        pl.semaphore_signal(sem, inc=1, device_id=peer, device_id_type=MESH)
    count += len(early.to) + len(early.frm)
    p = p_ref[...]
    src1[0:n, :] = mm(p, p, TN)
    src1[n:, :] = p[0:n, :] * jnp.where(row == 0, 1.0, 0.0)
    pl.semaphore_wait(sem, count)

    red = Reduce(out1, red1[0], red1[1], red1[2:], ncol)
    red.start_x(src1)
    early.start_one()
    red.start_z()
    red.start_c()
    early.start_two()
    red.finish()
    with_identity(work, out1[0:n, :])
    chol_inv(work, rows)
    l1, l1i = factors(rows)
    l1_ref[...] = l1

    xr = mm(p_ref[...], l1i, NT)
    src2[...] = mm(xr, xr, TN)
    red = Reduce(out2, red2[0], red2[1], red2[2:], ncol)
    red.start_x(src2)
    lead_ref[:, 0:n] = xr
    xt = mm(out1[n:, :], l1i, NT)
    load.wait()
    red.start_z()

    def block(k):
        early.block(k)
        xk = mm(pc[k], l1i, NT)
        vc_ref[k] = xk
        return mm3(halves(av[:, k * height:(k + 1) * height]), halves(xk))

    acc = block(0)
    acc = acc + block(1)
    red.start_c()
    acc = acc + block(2)
    acc = acc + block(3)
    yp[...] = acc
    early.finish()
    sl = height // ncol
    gc = red.gc

    def part(d):
        return pl.ds(pl.multiple_of(((c + d) % ncol) * sl, 8), sl)

    def wsend(d):
        return pltpu.make_async_remote_copy(
            src_ref=av.at[d * sl:(d + 1) * sl, 0:n], dst_ref=wbuf, send_sem=ws.at[d], recv_sem=wr,
            device_id=gc[d], device_id_type=MESH)

    ybuf[0] = yp[part(0), :]
    ysends = [send(yp.at[part(d), :], ybuf.at[d], ys.at[d], yr.at[d], gc[d]) for d in range(1, ncol)]

    @pl.when(c == 0)
    def _():
        for d in range(1, ncol):
            wsend(d).start()
        wbuf[...] = av[0:sl, 0:n]

    red.finish()
    fsends = []

    def share():
        for copy in ysends:
            copy.wait_recv()

        @pl.when(c != 0)
        def _():
            wsend(1).wait_recv()

        yw[part(0), 0:n] = slot_sum(ybuf, c, ncol)
        yw[part(0), n:] = wbuf[...]
        own = yw.at[part(0), :]
        fsends.extend(send(own, own, fs.at[d], fr.at[d], gc[d]) for d in range(1, ncol))

    with_identity(work, out2[...])
    chol_inv(work, rows, {4: share})
    l2, l2i = factors(rows)
    for d in range(1, ncol):
        theirs = yw.at[part(ncol - d), :]
        pltpu.make_async_remote_copy(
            src_ref=theirs, dst_ref=theirs, send_sem=fs.at[d], recv_sem=fr.at[d],
            device_id=gc[d], device_id_type=MESH).wait_recv()

    avr[...] = mm(yw[:, 0:n], l2i, NT) + yw[:, n:]
    late.start_one()
    vr = mm(lead_ref[:, 0:n], l2i, NT) + jnp.where(eyes((height, n), row * height), 1.0, 0.0)
    src3[...] = mm(vr, avr[...], TN)
    red = Reduce(out3, red3[0], red3[1], red3[2:], ncol)
    red.start_x(src3)
    with_identity(work, mm(xt, l2i, NT).T + jnp.where(eyes((n, n)), 1.0, 0.0))
    gj_inverse(work, {3: red.start_z})
    k = work[:, n:]
    red.start_c()
    late.start_two()
    for j in range(4):
        shift = (c * 4 + j) * height
        vc_ref[j] = mm(vc_ref[j], l2i, NT) + jnp.where(eyes((height, n), shift), 1.0, 0.0)
    band_ref[...] = -mm(l2, l1_ref[...], (((0,), (1,)), ((), ())))
    red.finish()
    inner = mm(k, mm(out3[...], k), TN)
    right = jnp.concatenate([
        jnp.concatenate([jnp.zeros((n, n), F32), k], axis=1),
        jnp.concatenate([k.T, -0.5 * (inner + inner.T)], axis=1)], axis=0)
    lead_ref[...] = mm(jnp.concatenate([avr[...], vr], axis=1), right)
    for j in range(4):
        late.block(j)
    late.finish()
    for copy in ysends + fsends:
        copy.wait_send()

    @pl.when(c == 0)
    def _():
        for d in range(1, ncol):
            wsend(d).wait_send()


def last_kernel(l1_in, band_in, lead_ref, avc_ref, vc_ref, a_ref, out_ref, band_ref, l1_ref, abuf, obuf, insem, outsem):
    width = avc_ref.shape[1]
    loads = [pltpu.make_async_copy(a_ref.at[:, k * width:(k + 1) * width], abuf.at[k], insem.at[k]) for k in range(4)]
    for copy in loads:
        copy.start()
    band_ref[...] = band_in[...]
    l1_ref[...] = l1_in[...]
    lead = halves(lead_ref[...])
    stores = []
    for k in range(4):
        tail = halves(jnp.concatenate([avc_ref[k], vc_ref[k]], axis=1))
        prod = mm3(lead, tail, NT)
        loads[k].wait()
        obuf[k] = abuf[k] - prod
        copy = pltpu.make_async_copy(obuf.at[k], out_ref.at[:, k * width:(k + 1) * width], outsem.at[k])
        copy.start()
        stores.append(copy)
    for copy in stores:
        copy.wait()


def body(ncol, panel, trailing):
    n = panel.shape[1]
    height, width = trailing.shape
    sl = height // ncol
    dma = pltpu.SemaphoreType.DMA

    def vmem(*shape):
        return pltpu.VMEM(shape, F32)

    l1, band, lead, avc, vc = pl.pallas_call(
        functools.partial(main_kernel, ncol),
        out_shape=(struct(n, n), struct(n, n), struct(height, 2 * n), struct(4, height, n), struct(4, height, n)),
        in_specs=[VM, ANY], out_specs=(VM,) * 5,
        scratch_shapes=[vmem(2 * n, n), vmem(2 * n, n), vmem(n, n), vmem(n, n), vmem(n, n), vmem(n, n)]
        + reduce_scratch(2 * n, ncol) + reduce_scratch(n, ncol) + reduce_scratch(n, ncol)
        + gather_sems() + gather_sems()
        + [vmem(height, width), vmem(4, height, n), vmem(n, 2 * n), vmem(n, 2 * n), vmem(height, n),
           vmem(ncol, sl, n), vmem(sl, n), vmem(height, 2 * n), vmem(height, n)]
        + [dma, dma((ncol,)), dma((ncol,)), dma((ncol,)), dma, dma((ncol,)), dma((ncol,))],
        compiler_params=pltpu.CompilerParams(collective_id=0, has_side_effects=True, vmem_limit_bytes=60 << 20),
        name="main")(panel, trailing)
    reduced, band, l1 = pl.pallas_call(
        last_kernel, out_shape=(struct(height, width), struct(n, n), struct(n, n)),
        in_specs=[VM] * 5 + [ANY], out_specs=(ANY, VM, VM),
        scratch_shapes=[vmem(4, height, width // 4), vmem(4, height, width // 4), dma((4,)), dma((4,))],
        compiler_params=pltpu.CompilerParams(vmem_limit_bytes=60 << 20), name="last",
    )(l1, band, lead, avc, vc, trailing)
    return reduced, band, l1


def solution(mesh):
    return jax.shard_map(
        functools.partial(body, mesh.shape["col"]), mesh=mesh, in_specs=(P("row", None), P("row", "col")),
        out_specs=(P("row", "col"), P(), P()), check_vma=False)
```

time: 1030 us -> 97.1 us (0.09)
  waiting for transfers between devices: 726 us -> 0 us
  other arithmetic: 166 us -> 0 us
  Pallas kernels: 0 us -> 95.6 us
  local copies, waits for them, and re-layouts: 79.2 us -> 0 us
  matrix products: 37.4 us -> 0 us
  between operations: 14.5 us -> 0.8 us
    psum x5 -> x0, waiting for transfers between devices: 627 us -> none  [the longest x1 144 us: body(): first_gram = lax.psum(gram_of(panel_block), 'row')]
    div x130 -> x0, other arithmetic: 107 us -> none  [the longest x128 106 us: eliminate(): pivot_row = pivot_row / pivot_row[pivot]]
    all_gather x2 -> x0, waiting for transfers between devices: 98.8 us -> none  [the longest x1 98.7 us: body(): all_update = lax.all_gather(row_update, 'row', axis=0, tiled=True)]
    pallas_call x0 -> x2, Pallas kernels: none -> 95.6 us  [the longest x1 88.6 us: body(): pl.pallas_call(functools.partial(main_kernel, ncol), out_shape=(struct(n,...]
    dynamic_slice x128 -> x0, local copies, waits for them, and re-layouts: 74.9 us -> none  [eliminate(): pivot_row = pivot_row / pivot_row[pivot]]
    another operation x10 -> x0, other arithmetic: 45.6 us -> none  [the longest x4 20.8 us: right_solve(): lax.linalg.triangular_solve(factor, values, left_side=False, lower=True,...]
    dot_general x52 -> x0, matrix products: 35.8 us -> none  [the longest x47 20.8 us: times_of(): jnp.dot(left, right, precision=HIGH, preferred_element_type=jnp.float32)]
  transfers between devices with their start and end apart: 7 -> 0, of which waited for: 6 -> 0; matrix products, arithmetic and copies ran while one was open for 20% -> 0% of each run, Pallas kernels for 0% -> 0%
where the time goes in v2:
time: 97.1 us; the launch traced here: 96.4 us
  Pallas kernels  95.6 us (98%)
    pallas_call x1, Pallas kernels, body(): pl.pallas_call(functools.partial(main_kernel, ncol), out_shape=(struct(n,...  88.6 us
    pallas_call x1, Pallas kernels, body(): pl.pallas_call(last_kernel, out_shape=(struct(height, width), struct(n, n...  6.98 us

profile of v2, /device:TPU:1, one launch (start us, length us, event | category | flops | bytes accessed | tf_op | source)
XLA Modules:
  0.0 96.4 jit_solution(15197526542430149285)
XLA Ops:
  0.6 88.6 %main.1 = (f32[128,128]{1,0:T(8,128)}, f32[128,128]{1,0:T(8,128)}, f32[512,256]{1,0:T(8,128)}, f32[4,512,128]{2,1,0:T(8,128)}, f32[4,512,128]{2,1,0:T(8,128)}) custom-call(f32[512,128]{1,0:T(8,128)} %p_ref.1, f32[512,2048]{1,0:T(8,128)} %a_ref.3), custom_call_target="tpu_custom_call" | custom-call | tf_op jit(solution)/shard_map/main/pallas_call | solution.py:439
  89.2 7.0 %last.1 = (f32[512,2048]{1,0:T(8,128)}, f32[128,128]{1,0:T(8,128)}, f32[128,128]{1,0:T(8,128)}) custom-call(f32[128,128]{1,0:T(8,128)} %get-tuple-element.8.l1_in, f32[128,128]{1,0:T(8,128)} %get-tuple-element.9.band_in, f32[512,256]{1,0:T(8,128)} %get-tuple-element.10.lead_ref, f32[4,512,128]{2,1,0:T(8,128)} %get-tuple-element.11.avc_ref, ...), custom_call_target="tpu_custom_call" | custom-call | tf_op jit(solution)/shard_map/last/pallas_call | solution.py:451

commit v3 on v2

--- a/solution.py
+++ b/solution.py
@@ -210,7 +210,8 @@
 class Gather:
     def __init__(self, src, out, sems, ncol):
         self.src, self.out = src, out
-        self.s1, self.r1, self.s2, self.r2 = sems
+        self.s1, self.r1, self.s2, self.r2, self.s3, self.r3 = sems
+        self.two = []
         self.x, self.z, self.c = place()
         y, core = self.c // 2, self.c % 2
         self.quarter = src.shape[0] // NX
@@ -229,22 +230,39 @@
         self.one = [send(self.src.at[self.rows(self.xd), :], self.out.at[k, self.rows(self.xd), :],
                          self.s1.at[j], self.r1.at[k], self.to[j]) for j in range(4)]
 
-    def start_two(self):
-        self.two = []
-        for j in range(4):
-            k = (self.z + j) % 4
-            part = self.out.at[k, self.rows(self.x), :]
-            pltpu.make_async_remote_copy(
-                src_ref=part, dst_ref=part, send_sem=self.s1.at[j], recv_sem=self.r1.at[k],
-                device_id=self.frm[0], device_id_type=MESH).wait_recv()
-            self.two += [send(part, part, self.s2.at[d, j], self.r2.at[d, k], self.gx[d]) for d in range(1, NX)]
+    def arrived(self, x, k, sem, lo=0, count=None):
+        rows = self.rows(x) if count is None else pl.ds(pl.multiple_of(x * self.quarter + lo, 8), count)
+        part = self.out.at[k, rows, :]
+        pltpu.make_async_remote_copy(
+            src_ref=part, dst_ref=part, send_sem=self.s1.at[0], recv_sem=sem,
+            device_id=self.frm[0], device_id_type=MESH).wait_recv()
+        return part
+
+    def nearest(self, j):
+        return (self.z + j) % 4
+
+    def forward(self, j, steps=(1, 2, 3)):
+        k = self.nearest(j)
+        part = self.arrived(self.x, k, self.r1.at[k])
+        self.two += [send(part, part, self.s2.at[d, j], self.r2.at[d, k], self.gx[d]) for d in steps]
+
+    def relay(self, j):
+        k = self.nearest(j)
+        half = self.quarter // 2
+        for i, d in enumerate((1, 3)):
+            x = (self.x + NX - d) % NX
+            self.arrived(x, k, self.r2.at[d, k])
+            part = self.out.at[k, pl.ds(pl.multiple_of(x * self.quarter + i * half, 8), half), :]
+            self.two.append(send(part, part, self.s3.at[i, j], self.r3.at[i, k], self.gx[d]))
 
     def block(self, k):
         for d in range(1, NX):
-            part = self.out.at[k, self.rows((self.x + NX - d) % NX), :]
-            pltpu.make_async_remote_copy(
-                src_ref=part, dst_ref=part, send_sem=self.s2.at[d, k], recv_sem=self.r2.at[d, k],
-                device_id=self.gx[d], device_id_type=MESH).wait_recv()
+            self.arrived((self.x + NX - d) % NX, k, self.r2.at[d, k])
+
+    def relayed(self, k):
+        half = self.quarter // 2
+        for i in range(2):
+            self.arrived((self.x + 2) % NX, k, self.r3.at[i, k], i * half, half)
 
     def finish(self):
         for copy in self.one + self.two:
@@ -253,7 +271,7 @@
 
 def gather_sems():
     dma = pltpu.SemaphoreType.DMA
-    return [dma((4,)), dma((4,)), dma((NX, 4)), dma((NX, 4))]
+    return [dma((4,)), dma((4,)), dma((NX, 4)), dma((NX, 4)), dma((2, 4)), dma((2, 4))]
 
 
 VM = pl.BlockSpec(memory_space=pltpu.VMEM)
@@ -264,7 +282,7 @@
     return jax.ShapeDtypeStruct(shape, F32)
 
 
-def main_kernel(ncol, p_ref, a_ref, l1_ref, band_ref, lead_ref, avc_ref, vc_ref, *scratch):
+def main_kernel(ncol, p_hbm, a_ref, l1_out, band_out, lead_out, avc_out, vc_out, *scratch):
     scratch = list(scratch)
 
     def take(count):
@@ -274,45 +292,94 @@
 
     src1, out1, src2, out2, src3, out3 = take(6)
     red1, red2, red3 = take(8), take(8), take(8)
-    gs1, gs2 = take(4), take(4)
+    gs1, gs2 = take(6), take(6)
     av, pc, work, rows, yp, ybuf, wbuf, yw, avr = take(9)
-    asem, ys, yr, ws, wr, fs, fr = take(7)
+    p_ref, l1_ref, band_ref, lead_ref, avc_ref, vc_ref = take(6)
+    asem, psem, osem, ys, yr, ws, wr, vs, vr_sem, fs, fr = take(11)
     n = p_ref.shape[1]
     height = p_ref.shape[0]
+    sl = height // ncol
     row, c = lax.axis_index("row"), lax.axis_index("col")
 
-    load = pltpu.make_async_copy(a_ref, av, asem)
-    load.start()
     sem, count = greet(ncol)
     early = Gather(p_ref, pc, gs1, ncol)
     late = Gather(avr, avc_ref, gs2, ncol)
     for peer in early.to + early.frm:
         pl.semaphore_signal(sem, inc=1, device_id=peer, device_id_type=MESH)
     count += len(early.to) + len(early.frm)
+    fetch = pltpu.make_async_copy(p_hbm, p_ref, psem)
+    fetch.start()
+    load = pltpu.make_async_copy(a_ref, av, asem)
+    load.start()
+    outs = []
+
+    def put(src, dst):
+        copy = pltpu.make_async_copy(src, dst, osem.at[len(outs)])
+        copy.start()
+        outs.append(copy)
+
+    fetch.wait()
     p = p_ref[...]
     src1[0:n, :] = mm(p, p, TN)
     src1[n:, :] = p[0:n, :] * jnp.where(row == 0, 1.0, 0.0)
     pl.semaphore_wait(sem, count)
 
     red = Reduce(out1, red1[0], red1[1], red1[2:], ncol)
+    gc = red.gc
     red.start_x(src1)
     early.start_one()
     red.start_z()
     red.start_c()
-    early.start_two()
+    for j in range(4):
+        early.forward(j)
     red.finish()
+
+    def part(d):
+        return pl.ds(pl.multiple_of(((c + d) % ncol) * sl, 8), sl)
+
+    def wsend(d):
+        return pltpu.make_async_remote_copy(
+            src_ref=av.at[d * sl:(d + 1) * sl, 0:n], dst_ref=wbuf, send_sem=ws.at[d], recv_sem=wr,
+            device_id=gc[d], device_id_type=MESH)
+
+    def share(lanes, ssems, rsems):
+        own = yw.at[part(0), lanes]
+        return [send(own, own, ssems.at[d], rsems.at[d], gc[d]) for d in range(1, ncol)]
+
+    def shared(lanes, ssems, rsems):
+        for d in range(1, ncol):
+            theirs = yw.at[part(ncol - d), lanes]
+            pltpu.make_async_remote_copy(
+                src_ref=theirs, dst_ref=theirs, send_sem=ssems.at[d], recv_sem=rsems.at[d],
+                device_id=gc[d], device_id_type=MESH).wait_recv()
+
+    load.wait()
+
+    @pl.when(c == 0)
+    def _():
+        for d in range(1, ncol):
+            wsend(d).start()
+        wbuf[...] = av[0:sl, 0:n]
+
     with_identity(work, out1[0:n, :])
     chol_inv(work, rows)
     l1, l1i = factors(rows)
-    l1_ref[...] = l1
 
     xr = mm(p_ref[...], l1i, NT)
     src2[...] = mm(xr, xr, TN)
     red = Reduce(out2, red2[0], red2[1], red2[2:], ncol)
     red.start_x(src2)
+    l1_ref[...] = l1
+    put(l1_ref, l1_out)
     lead_ref[:, 0:n] = xr
     xt = mm(out1[n:, :], l1i, NT)
-    load.wait()
+
+    @pl.when(c != 0)
+    def _():
+        wsend(1).wait_recv()
+
+    yw[part(0), n:] = wbuf[...]
+    wsends = share(slice(n, 2 * n), vs, vr_sem)
     red.start_z()
 
     def block(k):
@@ -323,55 +390,27 @@
 
     acc = block(0)
     acc = acc + block(1)
+    acc = acc + block(2)
     red.start_c()
-    acc = acc + block(2)
     acc = acc + block(3)
     yp[...] = acc
     early.finish()
-    sl = height // ncol
-    gc = red.gc
-
-    def part(d):
-        return pl.ds(pl.multiple_of(((c + d) % ncol) * sl, 8), sl)
-
-    def wsend(d):
-        return pltpu.make_async_remote_copy(
-            src_ref=av.at[d * sl:(d + 1) * sl, 0:n], dst_ref=wbuf, send_sem=ws.at[d], recv_sem=wr,
-            device_id=gc[d], device_id_type=MESH)
-
     ybuf[0] = yp[part(0), :]
     ysends = [send(yp.at[part(d), :], ybuf.at[d], ys.at[d], yr.at[d], gc[d]) for d in range(1, ncol)]
-
-    @pl.when(c == 0)
-    def _():
-        for d in range(1, ncol):
-            wsend(d).start()
-        wbuf[...] = av[0:sl, 0:n]
-
     red.finish()
     fsends = []
 
-    def share():
+    def spread():
         for copy in ysends:
             copy.wait_recv()
-
-        @pl.when(c != 0)
-        def _():
-            wsend(1).wait_recv()
-
         yw[part(0), 0:n] = slot_sum(ybuf, c, ncol)
-        yw[part(0), n:] = wbuf[...]
-        own = yw.at[part(0), :]
-        fsends.extend(send(own, own, fs.at[d], fr.at[d], gc[d]) for d in range(1, ncol))
+        fsends.extend(share(slice(0, n), fs, fr))
 
     with_identity(work, out2[...])
-    chol_inv(work, rows, {4: share})
+    chol_inv(work, rows, {3: spread})
     l2, l2i = factors(rows)
-    for d in range(1, ncol):
-        theirs = yw.at[part(ncol - d), :]
-        pltpu.make_async_remote_copy(
-            src_ref=theirs, dst_ref=theirs, send_sem=fs.at[d], recv_sem=fr.at[d],
-            device_id=gc[d], device_id_type=MESH).wait_recv()
+    shared(slice(n, 2 * n), vs, vr_sem)
+    shared(slice(0, n), fs, fr)
 
     avr[...] = mm(yw[:, 0:n], l2i, NT) + yw[:, n:]
     late.start_one()
@@ -380,24 +419,37 @@
     red = Reduce(out3, red3[0], red3[1], red3[2:], ncol)
     red.start_x(src3)
     with_identity(work, mm(xt, l2i, NT).T + jnp.where(eyes((n, n)), 1.0, 0.0))
-    gj_inverse(work, {3: red.start_z})
+    near = (1, 3)
+    gj_inverse(work, {4: red.start_z, 6: lambda: late.forward(0, near)})
     k = work[:, n:]
+    for j in range(1, 4):
+        late.forward(j, near)
     red.start_c()
-    late.start_two()
     for j in range(4):
         shift = (c * 4 + j) * height
         vc_ref[j] = mm(vc_ref[j], l2i, NT) + jnp.where(eyes((height, n), shift), 1.0, 0.0)
+        put(vc_ref.at[j], vc_out.at[j])
     band_ref[...] = -mm(l2, l1_ref[...], (((0,), (1,)), ((), ())))
+    put(band_ref, band_out)
+    late.relay(0)
+    late.relay(1)
     red.finish()
     inner = mm(k, mm(out3[...], k), TN)
     right = jnp.concatenate([
         jnp.concatenate([jnp.zeros((n, n), F32), k], axis=1),
         jnp.concatenate([k.T, -0.5 * (inner + inner.T)], axis=1)], axis=0)
     lead_ref[...] = mm(jnp.concatenate([avr[...], vr], axis=1), right)
+    put(lead_ref, lead_out)
+    late.relay(2)
+    late.relay(3)
     for j in range(4):
-        late.block(j)
+        at = late.nearest(j)
+        late.relayed(at)
+        put(avc_ref.at[at], avc_out.at[at])
     late.finish()
-    for copy in ysends + fsends:
+    for copy in outs:
+        copy.wait()
+    for copy in ysends + fsends + wsends:
         copy.wait_send()
 
     @pl.when(c == 0)
@@ -406,23 +458,38 @@
             wsend(d).wait_send()
 
 
-def last_kernel(l1_in, band_in, lead_ref, avc_ref, vc_ref, a_ref, out_ref, band_ref, l1_ref, abuf, obuf, insem, outsem):
-    width = avc_ref.shape[1]
-    loads = [pltpu.make_async_copy(a_ref.at[:, k * width:(k + 1) * width], abuf.at[k], insem.at[k]) for k in range(4)]
-    for copy in loads:
-        copy.start()
+def last_kernel(l1_in, band_in, lead_in, avc_in, vc_in, a_ref, out_ref, band_ref, l1_ref,
+                lead_ref, pairs, abuf, obuf, leadsem, insem, outsem):
+    parts, height, n = avc_in.shape
+    width = height // 2
+    first = pltpu.make_async_copy(lead_in, lead_ref, leadsem)
+    first.start()
+    loads = []
+    for k in range(parts):
+        loads.append([
+            pltpu.make_async_copy(avc_in.at[k], pairs.at[k, :, 0:n], insem.at[k, 0]),
+            pltpu.make_async_copy(vc_in.at[k], pairs.at[k, :, n:2 * n], insem.at[k, 1]),
+            pltpu.make_async_copy(a_ref.at[:, k * height:(k + 1) * height], abuf.at[k], insem.at[k, 2])])
+        for copy in loads[k]:
+            copy.start()
     band_ref[...] = band_in[...]
     l1_ref[...] = l1_in[...]
+    first.wait()
     lead = halves(lead_ref[...])
     stores = []
-    for k in range(4):
-        tail = halves(jnp.concatenate([avc_ref[k], vc_ref[k]], axis=1))
-        prod = mm3(lead, tail, NT)
-        loads[k].wait()
-        obuf[k] = abuf[k] - prod
-        copy = pltpu.make_async_copy(obuf.at[k], out_ref.at[:, k * width:(k + 1) * width], outsem.at[k])
-        copy.start()
-        stores.append(copy)
+    for k in range(parts):
+        loads[k][0].wait()
+        loads[k][1].wait()
+        for h in range(2):
+            cols = slice(h * width, (h + 1) * width)
+            prod = mm3(lead, halves(pairs[k, cols, :]), NT)
+            if h == 0:
+                loads[k][2].wait()
+            obuf[k, :, cols] = abuf[k, :, cols] - prod
+            at = k * height + h * width
+            copy = pltpu.make_async_copy(obuf.at[k, :, cols], out_ref.at[:, at:at + width], outsem.at[k, h])
+            copy.start()
+            stores.append(copy)
     for copy in stores:
         copy.wait()
 
@@ -439,19 +506,22 @@
     l1, band, lead, avc, vc = pl.pallas_call(
         functools.partial(main_kernel, ncol),
         out_shape=(struct(n, n), struct(n, n), struct(height, 2 * n), struct(4, height, n), struct(4, height, n)),
-        in_specs=[VM, ANY], out_specs=(VM,) * 5,
+        in_specs=[ANY, ANY], out_specs=(ANY,) * 5,
         scratch_shapes=[vmem(2 * n, n), vmem(2 * n, n), vmem(n, n), vmem(n, n), vmem(n, n), vmem(n, n)]
         + reduce_scratch(2 * n, ncol) + reduce_scratch(n, ncol) + reduce_scratch(n, ncol)
         + gather_sems() + gather_sems()
         + [vmem(height, width), vmem(4, height, n), vmem(n, 2 * n), vmem(n, 2 * n), vmem(height, n),
-           vmem(ncol, sl, n), vmem(sl, n), vmem(height, 2 * n), vmem(height, n)]
-        + [dma, dma((ncol,)), dma((ncol,)), dma((ncol,)), dma, dma((ncol,)), dma((ncol,))],
+           vmem(ncol, sl, n), vmem(sl, n), vmem(height, 2 * n), vmem(height, n),
+           vmem(height, n), vmem(n, n), vmem(n, n), vmem(height, 2 * n), vmem(4, height, n), vmem(4, height, n)]
+        + [dma, dma, dma((16,)), dma((ncol,)), dma((ncol,)), dma((ncol,)), dma]
+        + [dma((ncol,)), dma((ncol,)), dma((ncol,)), dma((ncol,))],
         compiler_params=pltpu.CompilerParams(collective_id=0, has_side_effects=True, vmem_limit_bytes=60 << 20),
         name="main")(panel, trailing)
     reduced, band, l1 = pl.pallas_call(
         last_kernel, out_shape=(struct(height, width), struct(n, n), struct(n, n)),
-        in_specs=[VM] * 5 + [ANY], out_specs=(ANY, VM, VM),
-        scratch_shapes=[vmem(4, height, width // 4), vmem(4, height, width // 4), dma((4,)), dma((4,))],
+        in_specs=[VM] * 2 + [ANY] * 4, out_specs=(ANY, VM, VM),
+        scratch_shapes=[vmem(height, 2 * n), vmem(4, height, 2 * n), vmem(4, height, width // 4), vmem(4, height, width // 4),
+                        dma, dma((4, 3)), dma((4, 2))],
         compiler_params=pltpu.CompilerParams(vmem_limit_bytes=60 << 20), name="last",
     )(l1, band, lead, avc, vc, trailing)
     return reduced, band, l1

time: 97.1 us -> 90.8 us (0.935)
  Pallas kernels: 95.6 us -> 89.3 us
    pallas_call x1, Pallas kernels: 88.6 us -> 79.3 us  [body(): pl.pallas_call(functools.partial(main_kernel, ncol), out_shape=(struct(n,...]
    pallas_call x1, Pallas kernels: 6.98 us -> 9.96 us  [body(): pl.pallas_call(last_kernel, out_shape=(struct(height, width), struct(n, n...]
where the time goes in v3:
time: 90.8 us; the launch traced here: 90.1 us
  Pallas kernels  89.3 us (98%)
    pallas_call x1, Pallas kernels, body(): pl.pallas_call(functools.partial(main_kernel, ncol), out_shape=(struct(n,...  79.3 us
    pallas_call x1, Pallas kernels, body(): pl.pallas_call(last_kernel, out_shape=(struct(height, width), struct(n, n...  9.96 us

profile of v3, /device:TPU:1, one launch (start us, length us, event | category | flops | bytes accessed | tf_op | source)
XLA Modules:
  0.0 90.1 jit_solution(12409557347441739690)
XLA Ops:
  0.6 79.3 %main.1 = (f32[128,128]{1,0:T(8,128)}, f32[128,128]{1,0:T(8,128)}, f32[512,256]{1,0:T(8,128)}, f32[4,512,128]{2,1,0:T(8,128)}, f32[4,512,128]{2,1,0:T(8,128)}) custom-call(f32[512,128]{1,0:T(8,128)} %p_hbm.1, f32[512,2048]{1,0:T(8,128)} %a_ref.3), custom_call_target="tpu_custom_call" | custom-call | tf_op jit(solution)/shard_map/main/pallas_call | solution.py:506
  80.0 10.0 %last.1 = (f32[512,2048]{1,0:T(8,128)}, f32[128,128]{1,0:T(8,128)}, f32[128,128]{1,0:T(8,128)}) custom-call(f32[128,128]{1,0:T(8,128)} %get-tuple-element.8.l1_in, f32[128,128]{1,0:T(8,128)} %get-tuple-element.9.band_in, f32[512,256]{1,0:T(8,128)} %get-tuple-element.10.lead_in, f32[4,512,128]{2,1,0:T(8,128)} %get-tuple-element.11.avc_in, ...), custom_call_target="tpu_custom_call" | custom-call | tf_op jit(solution)/shard_map/last/pallas_call | solution.py:520

commit v4 on v3

--- a/solution.py
+++ b/solution.py
@@ -142,6 +142,16 @@
     return total
 
 
+def all_in(view, sem, peer):
+    pltpu.make_async_remote_copy(
+        src_ref=view, dst_ref=view, send_sem=sem, recv_sem=sem, device_id=peer, device_id_type=MESH).wait_recv()
+
+
+def all_out(view, sem, peer):
+    pltpu.make_async_remote_copy(
+        src_ref=view, dst_ref=view, send_sem=sem, recv_sem=sem, device_id=peer, device_id_type=MESH).wait_send()
+
+
 class Reduce:
     def __init__(self, out, xbuf, zbuf, sems, ncol):
         self.out, self.xbuf, self.zbuf, self.ncol = out, xbuf, zbuf, ncol
@@ -149,46 +159,41 @@
         self.gx, self.gz, self.gc = groups(ncol)
         self.x, self.z, self.c = place()
         self.sl = out.shape[0] // ncol
-        self.open = []
 
     def part(self):
         return pl.ds(pl.multiple_of(self.c * self.sl, 8), self.sl)
 
     def start_x(self, src):
         self.xbuf[0] = src[self.part(), :]
-        self.now = [send(self.xbuf.at[0], self.xbuf.at[d], self.xs.at[d], self.xr.at[d], self.gx[d]) for d in range(1, NX)]
+        for d in range(1, NX):
+            send(self.xbuf.at[0], self.xbuf.at[d], self.xs, self.xr, self.gx[d])
 
     def start_z(self):
-        for copy in self.now:
-            copy.wait_recv()
-        self.open += self.now
+        all_in(self.xbuf.at[1:NX], self.xr, self.gx[1])
         self.zbuf[0] = slot_sum(self.xbuf, self.x, NX)
-        self.now = [send(self.zbuf.at[0], self.zbuf.at[d], self.zs.at[d], self.zr.at[d], self.gz[d]) for d in range(1, NZ)]
+        for d in range(1, NZ):
+            send(self.zbuf.at[0], self.zbuf.at[d], self.zs, self.zr, self.gz[d])
 
     def start_c(self):
-        for copy in self.now:
-            copy.wait_recv()
-        self.open += self.now
+        all_in(self.zbuf.at[1:NZ], self.zr, self.gz[1])
         self.out[self.part(), :] = slot_sum(self.zbuf, self.z, NZ)
         mine = self.out.at[self.part(), :]
-        self.now = [send(mine, mine, self.cs.at[d], self.cr.at[d], self.gc[d]) for d in range(1, self.ncol)]
+        for d in range(1, self.ncol):
+            send(mine, mine, self.cs, self.cr, self.gc[d])
 
     def finish(self):
-        for d, copy in enumerate(self.now, 1):
-            rows = pl.ds(pl.multiple_of(((self.c + self.ncol - d) % self.ncol) * self.sl, 8), self.sl)
-            theirs = self.out.at[rows, :]
-            pltpu.make_async_remote_copy(
-                src_ref=theirs, dst_ref=theirs, send_sem=self.cs.at[d], recv_sem=self.cr.at[d],
-                device_id=self.gc[d], device_id_type=MESH).wait_recv()
-        for copy in self.open + self.now:
-            copy.wait_send()
+        rest = self.out.at[0:(self.ncol - 1) * self.sl, :]
+        all_in(rest, self.cr, self.gc[1])
+        all_out(self.xbuf.at[1:NX], self.xs, self.gx[1])
+        all_out(self.zbuf.at[1:NZ], self.zs, self.gz[1])
+        all_out(rest, self.cs, self.gc[1])
 
 
 def reduce_scratch(height, ncol):
     sl = height // ncol
     dma = pltpu.SemaphoreType.DMA
     return [pltpu.VMEM((NX, sl, 128), F32), pltpu.VMEM((NZ, sl, 128), F32),
-            dma((NX,)), dma((NX,)), dma((NZ,)), dma((NZ,)), dma((ncol,)), dma((ncol,))]
+            dma, dma, dma, dma, dma, dma]
 
 
 VM = pl.BlockSpec(memory_space=pltpu.VMEM)
@@ -211,7 +216,6 @@
     def __init__(self, src, out, sems, ncol):
         self.src, self.out = src, out
         self.s1, self.r1, self.s2, self.r2, self.s3, self.r3 = sems
-        self.two = []
         self.x, self.z, self.c = place()
         y, core = self.c // 2, self.c % 2
         self.quarter = src.shape[0] // NX
@@ -227,51 +231,45 @@
 
     def start_one(self):
         k = self.z % 4
-        self.one = [send(self.src.at[self.rows(self.xd), :], self.out.at[k, self.rows(self.xd), :],
-                         self.s1.at[j], self.r1.at[k], self.to[j]) for j in range(4)]
-
-    def arrived(self, x, k, sem, lo=0, count=None):
-        rows = self.rows(x) if count is None else pl.ds(pl.multiple_of(x * self.quarter + lo, 8), count)
-        part = self.out.at[k, rows, :]
-        pltpu.make_async_remote_copy(
-            src_ref=part, dst_ref=part, send_sem=self.s1.at[0], recv_sem=sem,
-            device_id=self.frm[0], device_id_type=MESH).wait_recv()
-        return part
+        for j in range(4):
+            send(self.src.at[self.rows(self.xd), :], self.out.at[k, self.rows(self.xd), :],
+                 self.s1, self.r1.at[k], self.to[j])
 
     def nearest(self, j):
         return (self.z + j) % 4
 
     def forward(self, j, steps=(1, 2, 3)):
         k = self.nearest(j)
-        part = self.arrived(self.x, k, self.r1.at[k])
-        self.two += [send(part, part, self.s2.at[d, j], self.r2.at[d, k], self.gx[d]) for d in steps]
+        part = self.out.at[k, self.rows(self.x), :]
+        all_in(part, self.r1.at[k], self.frm[0])
+        for d in steps:
+            send(part, part, self.s2, self.r2.at[k], self.gx[d])
 
     def relay(self, j):
         k = self.nearest(j)
         half = self.quarter // 2
+        all_in(self.out.at[k, 0:2 * self.quarter, :], self.r2.at[k], self.gx[1])
         for i, d in enumerate((1, 3)):
             x = (self.x + NX - d) % NX
-            self.arrived(x, k, self.r2.at[d, k])
             part = self.out.at[k, pl.ds(pl.multiple_of(x * self.quarter + i * half, 8), half), :]
-            self.two.append(send(part, part, self.s3.at[i, j], self.r3.at[i, k], self.gx[d]))
+            send(part, part, self.s3, self.r3.at[k], self.gx[d])
 
     def block(self, k):
-        for d in range(1, NX):
-            self.arrived((self.x + NX - d) % NX, k, self.r2.at[d, k])
+        all_in(self.out.at[k, 0:3 * self.quarter, :], self.r2.at[k], self.gx[1])
 
     def relayed(self, k):
-        half = self.quarter // 2
-        for i in range(2):
-            self.arrived((self.x + 2) % NX, k, self.r3.at[i, k], i * half, half)
-
-    def finish(self):
-        for copy in self.one + self.two:
-            copy.wait_send()
+        all_in(self.out.at[k, 0:self.quarter, :], self.r3.at[k], self.gx[1])
+
+    def finish(self, near):
+        all_out(self.out.at[:, 0:self.quarter, :], self.s1, self.to[0])
+        all_out(self.out.at[:, 0:near * self.quarter, :], self.s2, self.gx[1])
+        if near == 2:
+            all_out(self.out.at[:, 0:self.quarter, :], self.s3, self.gx[1])
 
 
 def gather_sems():
     dma = pltpu.SemaphoreType.DMA
-    return [dma((4,)), dma((4,)), dma((NX, 4)), dma((NX, 4)), dma((2, 4)), dma((2, 4))]
+    return [dma, dma((4,)), dma, dma((4,)), dma, dma((4,))]
 
 
 VM = pl.BlockSpec(memory_space=pltpu.VMEM)
@@ -327,31 +325,28 @@
     red = Reduce(out1, red1[0], red1[1], red1[2:], ncol)
     gc = red.gc
     red.start_x(src1)
+    red.start_z()
     early.start_one()
-    red.start_z()
     red.start_c()
+    red.finish()
     for j in range(4):
         early.forward(j)
-    red.finish()
 
     def part(d):
         return pl.ds(pl.multiple_of(((c + d) % ncol) * sl, 8), sl)
 
     def wsend(d):
         return pltpu.make_async_remote_copy(
-            src_ref=av.at[d * sl:(d + 1) * sl, 0:n], dst_ref=wbuf, send_sem=ws.at[d], recv_sem=wr,
+            src_ref=av.at[d * sl:(d + 1) * sl, 0:n], dst_ref=wbuf, send_sem=ws, recv_sem=wr,
             device_id=gc[d], device_id_type=MESH)
 
-    def share(lanes, ssems, rsems):
+    def share(lanes, ssem, rsem):
         own = yw.at[part(0), lanes]
-        return [send(own, own, ssems.at[d], rsems.at[d], gc[d]) for d in range(1, ncol)]
-
-    def shared(lanes, ssems, rsems):
         for d in range(1, ncol):
-            theirs = yw.at[part(ncol - d), lanes]
-            pltpu.make_async_remote_copy(
-                src_ref=theirs, dst_ref=theirs, send_sem=ssems.at[d], recv_sem=rsems.at[d],
-                device_id=gc[d], device_id_type=MESH).wait_recv()
+            send(own, own, ssem, rsem, gc[d])
+
+    def rest(lanes):
+        return yw.at[0:(ncol - 1) * sl, lanes]
 
     load.wait()
 
@@ -379,7 +374,7 @@
         wsend(1).wait_recv()
 
     yw[part(0), n:] = wbuf[...]
-    wsends = share(slice(n, 2 * n), vs, vr_sem)
+    share(slice(n, 2 * n), vs, vr_sem)
     red.start_z()
 
     def block(k):
@@ -394,45 +389,46 @@
     red.start_c()
     acc = acc + block(3)
     yp[...] = acc
-    early.finish()
+    early.finish(3)
     ybuf[0] = yp[part(0), :]
-    ysends = [send(yp.at[part(d), :], ybuf.at[d], ys.at[d], yr.at[d], gc[d]) for d in range(1, ncol)]
+    for d in range(1, ncol):
+        send(yp.at[part(d), :], ybuf.at[d], ys, yr, gc[d])
     red.finish()
-    fsends = []
 
     def spread():
-        for copy in ysends:
-            copy.wait_recv()
+        all_in(ybuf.at[1:ncol], yr, gc[1])
         yw[part(0), 0:n] = slot_sum(ybuf, c, ncol)
-        fsends.extend(share(slice(0, n), fs, fr))
+        share(slice(0, n), fs, fr)
 
     with_identity(work, out2[...])
-    chol_inv(work, rows, {3: spread})
+    chol_inv(work, rows, {1: spread})
     l2, l2i = factors(rows)
-    shared(slice(n, 2 * n), vs, vr_sem)
-    shared(slice(0, n), fs, fr)
+    vr = mm(lead_ref[:, 0:n], l2i, NT) + jnp.where(eyes((height, n), row * height), 1.0, 0.0)
+    with_identity(work, mm(xt, l2i, NT).T + jnp.where(eyes((n, n)), 1.0, 0.0))
+    for j in range(4):
+        shift = (c * 4 + j) * height
+        vc_ref[j] = mm(vc_ref[j], l2i, NT) + jnp.where(eyes((height, n), shift), 1.0, 0.0)
+        put(vc_ref.at[j], vc_out.at[j])
+    all_in(rest(slice(n, 2 * n)), vr_sem, gc[1])
+    all_in(rest(slice(0, n)), fr, gc[1])
 
     avr[...] = mm(yw[:, 0:n], l2i, NT) + yw[:, n:]
     late.start_one()
-    vr = mm(lead_ref[:, 0:n], l2i, NT) + jnp.where(eyes((height, n), row * height), 1.0, 0.0)
     src3[...] = mm(vr, avr[...], TN)
     red = Reduce(out3, red3[0], red3[1], red3[2:], ncol)
     red.start_x(src3)
-    with_identity(work, mm(xt, l2i, NT).T + jnp.where(eyes((n, n)), 1.0, 0.0))
     near = (1, 3)
     gj_inverse(work, {4: red.start_z, 6: lambda: late.forward(0, near)})
     k = work[:, n:]
     for j in range(1, 4):
         late.forward(j, near)
     red.start_c()
-    for j in range(4):
-        shift = (c * 4 + j) * height
-        vc_ref[j] = mm(vc_ref[j], l2i, NT) + jnp.where(eyes((height, n), shift), 1.0, 0.0)
-        put(vc_ref.at[j], vc_out.at[j])
+    late.relay(0)
+    late.relay(1)
     band_ref[...] = -mm(l2, l1_ref[...], (((0,), (1,)), ((), ())))
     put(band_ref, band_out)
-    late.relay(0)
-    late.relay(1)
+    late.relay(2)
+    late.relay(3)
     red.finish()
     inner = mm(k, mm(out3[...], k), TN)
     right = jnp.concatenate([
@@ -440,56 +436,39 @@
         jnp.concatenate([k.T, -0.5 * (inner + inner.T)], axis=1)], axis=0)
     lead_ref[...] = mm(jnp.concatenate([avr[...], vr], axis=1), right)
     put(lead_ref, lead_out)
-    late.relay(2)
-    late.relay(3)
     for j in range(4):
         at = late.nearest(j)
         late.relayed(at)
         put(avc_ref.at[at], avc_out.at[at])
-    late.finish()
+    late.finish(2)
     for copy in outs:
         copy.wait()
-    for copy in ysends + fsends + wsends:
-        copy.wait_send()
+    all_out(ybuf.at[1:ncol], ys, gc[1])
+    all_out(rest(slice(0, n)), fs, gc[1])
+    all_out(rest(slice(n, 2 * n)), vs, gc[1])
 
     @pl.when(c == 0)
     def _():
-        for d in range(1, ncol):
-            wsend(d).wait_send()
-
-
-def last_kernel(l1_in, band_in, lead_in, avc_in, vc_in, a_ref, out_ref, band_ref, l1_ref,
-                lead_ref, pairs, abuf, obuf, leadsem, insem, outsem):
-    parts, height, n = avc_in.shape
-    width = height // 2
-    first = pltpu.make_async_copy(lead_in, lead_ref, leadsem)
-    first.start()
-    loads = []
-    for k in range(parts):
-        loads.append([
-            pltpu.make_async_copy(avc_in.at[k], pairs.at[k, :, 0:n], insem.at[k, 0]),
-            pltpu.make_async_copy(vc_in.at[k], pairs.at[k, :, n:2 * n], insem.at[k, 1]),
-            pltpu.make_async_copy(a_ref.at[:, k * height:(k + 1) * height], abuf.at[k], insem.at[k, 2])])
-        for copy in loads[k]:
-            copy.start()
+        all_out(rest(slice(0, n)), ws, gc[1])
+
+
+def last_kernel(l1_in, band_in, lead_ref, avc_ref, vc_ref, a_ref, out_ref, band_ref, l1_ref, abuf, obuf, insem, outsem):
+    width = avc_ref.shape[1]
+    loads = [pltpu.make_async_copy(a_ref.at[:, k * width:(k + 1) * width], abuf.at[k], insem.at[k]) for k in range(4)]
+    for copy in loads:
+        copy.start()
     band_ref[...] = band_in[...]
     l1_ref[...] = l1_in[...]
-    first.wait()
     lead = halves(lead_ref[...])
     stores = []
-    for k in range(parts):
-        loads[k][0].wait()
-        loads[k][1].wait()
-        for h in range(2):
-            cols = slice(h * width, (h + 1) * width)
-            prod = mm3(lead, halves(pairs[k, cols, :]), NT)
-            if h == 0:
-                loads[k][2].wait()
-            obuf[k, :, cols] = abuf[k, :, cols] - prod
-            at = k * height + h * width
-            copy = pltpu.make_async_copy(obuf.at[k, :, cols], out_ref.at[:, at:at + width], outsem.at[k, h])
-            copy.start()
-            stores.append(copy)
+    for k in range(4):
+        tail = halves(jnp.concatenate([avc_ref[k], vc_ref[k]], axis=1))
+        prod = mm3(lead, tail, NT)
+        loads[k].wait()
+        obuf[k] = abuf[k] - prod
+        copy = pltpu.make_async_copy(obuf.at[k], out_ref.at[:, k * width:(k + 1) * width], outsem.at[k])
+        copy.start()
+        stores.append(copy)
     for copy in stores:
         copy.wait()
 
@@ -513,15 +492,13 @@
         + [vmem(height, width), vmem(4, height, n), vmem(n, 2 * n), vmem(n, 2 * n), vmem(height, n),
            vmem(ncol, sl, n), vmem(sl, n), vmem(height, 2 * n), vmem(height, n),
            vmem(height, n), vmem(n, n), vmem(n, n), vmem(height, 2 * n), vmem(4, height, n), vmem(4, height, n)]
-        + [dma, dma, dma((16,)), dma((ncol,)), dma((ncol,)), dma((ncol,)), dma]
-        + [dma((ncol,)), dma((ncol,)), dma((ncol,)), dma((ncol,))],
+        + [dma, dma, dma((11,)), dma, dma, dma, dma, dma, dma, dma, dma],
         compiler_params=pltpu.CompilerParams(collective_id=0, has_side_effects=True, vmem_limit_bytes=60 << 20),
         name="main")(panel, trailing)
     reduced, band, l1 = pl.pallas_call(
         last_kernel, out_shape=(struct(height, width), struct(n, n), struct(n, n)),
-        in_specs=[VM] * 2 + [ANY] * 4, out_specs=(ANY, VM, VM),
-        scratch_shapes=[vmem(height, 2 * n), vmem(4, height, 2 * n), vmem(4, height, width // 4), vmem(4, height, width // 4),
-                        dma, dma((4, 3)), dma((4, 2))],
+        in_specs=[VM] * 5 + [ANY], out_specs=(ANY, VM, VM),
+        scratch_shapes=[vmem(4, height, width // 4), vmem(4, height, width // 4), dma((4,)), dma((4,))],
         compiler_params=pltpu.CompilerParams(vmem_limit_bytes=60 << 20), name="last",
     )(l1, band, lead, avc, vc, trailing)
     return reduced, band, l1

time: 90.8 us -> 88.9 us (0.979)
  Pallas kernels: 89.3 us -> 87.9 us
    pallas_call x1, Pallas kernels: 9.96 us -> 7 us  [body(): pl.pallas_call(last_kernel, out_shape=(struct(height, width), struct(n, n...]
    pallas_call x1, Pallas kernels: 79.3 us -> 80.9 us  [body(): pl.pallas_call(functools.partial(main_kernel, ncol), out_shape=(struct(n,...]
where the time goes in v4:
time: 88.9 us; the launch traced here: 88.7 us
  Pallas kernels  87.9 us (99%)
    pallas_call x1, Pallas kernels, body(): pl.pallas_call(functools.partial(main_kernel, ncol), out_shape=(struct(n,...  80.9 us
    pallas_call x1, Pallas kernels, body(): pl.pallas_call(last_kernel, out_shape=(struct(height, width), struct(n, n...  7 us

profile of v4, /device:TPU:1, one launch (start us, length us, event | category | flops | bytes accessed | tf_op | source)
XLA Modules:
  0.0 88.7 jit_solution(14560099193119746208)
XLA Ops:
  0.6 80.9 %main.1 = (f32[128,128]{1,0:T(8,128)}, f32[128,128]{1,0:T(8,128)}, f32[512,256]{1,0:T(8,128)}, f32[4,512,128]{2,1,0:T(8,128)}, f32[4,512,128]{2,1,0:T(8,128)}) custom-call(f32[512,128]{1,0:T(8,128)} %p_hbm.1, f32[512,2048]{1,0:T(8,128)} %a_ref.3), custom_call_target="tpu_custom_call" | custom-call | tf_op jit(solution)/shard_map/main/pallas_call | solution.py:485
  81.6 7.0 %last.1 = (f32[512,2048]{1,0:T(8,128)}, f32[128,128]{1,0:T(8,128)}, f32[128,128]{1,0:T(8,128)}) custom-call(f32[128,128]{1,0:T(8,128)} %get-tuple-element.8.l1_in, f32[128,128]{1,0:T(8,128)} %get-tuple-element.9.band_in, f32[512,256]{1,0:T(8,128)} %get-tuple-element.10.lead_ref, f32[4,512,128]{2,1,0:T(8,128)} %get-tuple-element.11.avc_ref, ...), custom_call_target="tpu_custom_call" | custom-call | tf_op jit(solution)/shard_map/last/pallas_call | solution.py:498

commit v5 on v4

--- a/solution.py
+++ b/solution.py
@@ -153,30 +153,34 @@
 
 
 class Reduce:
-    def __init__(self, out, xbuf, zbuf, sems, ncol):
-        self.out, self.xbuf, self.zbuf, self.ncol = out, xbuf, zbuf, ncol
-        self.xs, self.xr, self.zs, self.zr, self.cs, self.cr = sems
-        self.gx, self.gz, self.gc = groups(ncol)
-        self.x, self.z, self.c = place()
+    def __init__(self, out, first, second, sems, ncol, z_first=False):
+        self.out, self.first, self.second, self.ncol = out, first, second, ncol
+        self.s1, self.r1, self.s2, self.r2, self.cs, self.cr = sems
+        gx, gz, self.gc = groups(ncol)
+        x, z, self.c = place()
+        self.g1, self.g2 = (gz, gx) if z_first else (gx, gz)
+        self.i1, self.i2 = (z, x) if z_first else (x, z)
         self.sl = out.shape[0] // ncol
 
     def part(self):
         return pl.ds(pl.multiple_of(self.c * self.sl, 8), self.sl)
 
-    def start_x(self, src):
-        self.xbuf[0] = src[self.part(), :]
-        for d in range(1, NX):
-            send(self.xbuf.at[0], self.xbuf.at[d], self.xs, self.xr, self.gx[d])
-
-    def start_z(self):
-        all_in(self.xbuf.at[1:NX], self.xr, self.gx[1])
-        self.zbuf[0] = slot_sum(self.xbuf, self.x, NX)
-        for d in range(1, NZ):
-            send(self.zbuf.at[0], self.zbuf.at[d], self.zs, self.zr, self.gz[d])
+    def start_first(self, src):
+        self.first[0] = src[self.part(), :]
+        for d in range(1, len(self.g1)):
+            send(self.first.at[0], self.first.at[d], self.s1, self.r1, self.g1[d])
+
+    def start_second(self):
+        count = len(self.g1)
+        all_in(self.first.at[1:count], self.r1, self.g1[1])
+        self.second[0] = slot_sum(self.first, self.i1, count)
+        for d in range(1, len(self.g2)):
+            send(self.second.at[0], self.second.at[d], self.s2, self.r2, self.g2[d])
 
     def start_c(self):
-        all_in(self.zbuf.at[1:NZ], self.zr, self.gz[1])
-        self.out[self.part(), :] = slot_sum(self.zbuf, self.z, NZ)
+        count = len(self.g2)
+        all_in(self.second.at[1:count], self.r2, self.g2[1])
+        self.out[self.part(), :] = slot_sum(self.second, self.i2, count)
         mine = self.out.at[self.part(), :]
         for d in range(1, self.ncol):
             send(mine, mine, self.cs, self.cr, self.gc[d])
@@ -184,8 +188,8 @@
     def finish(self):
         rest = self.out.at[0:(self.ncol - 1) * self.sl, :]
         all_in(rest, self.cr, self.gc[1])
-        all_out(self.xbuf.at[1:NX], self.xs, self.gx[1])
-        all_out(self.zbuf.at[1:NZ], self.zs, self.gz[1])
+        all_out(self.first.at[1:len(self.g1)], self.s1, self.g1[1])
+        all_out(self.second.at[1:len(self.g2)], self.s2, self.g2[1])
         all_out(rest, self.cs, self.gc[1])
 
 
@@ -324,13 +328,13 @@
 
     red = Reduce(out1, red1[0], red1[1], red1[2:], ncol)
     gc = red.gc
-    red.start_x(src1)
-    red.start_z()
+    red.start_first(src1)
+    red.start_second()
     early.start_one()
     red.start_c()
-    red.finish()
     for j in range(4):
         early.forward(j)
+    red.finish()
 
     def part(d):
         return pl.ds(pl.multiple_of(((c + d) % ncol) * sl, 8), sl)
@@ -362,8 +366,8 @@
 
     xr = mm(p_ref[...], l1i, NT)
     src2[...] = mm(xr, xr, TN)
-    red = Reduce(out2, red2[0], red2[1], red2[2:], ncol)
-    red.start_x(src2)
+    red = Reduce(out2, red2[1], red2[0], red2[2:], ncol, z_first=True)
+    red.start_first(src2)
     l1_ref[...] = l1
     put(l1_ref, l1_out)
     lead_ref[:, 0:n] = xr
@@ -375,7 +379,7 @@
 
     yw[part(0), n:] = wbuf[...]
     share(slice(n, 2 * n), vs, vr_sem)
-    red.start_z()
+    red.start_second()
 
     def block(k):
         early.block(k)
@@ -403,31 +407,38 @@
     with_identity(work, out2[...])
     chol_inv(work, rows, {1: spread})
     l2, l2i = factors(rows)
+    all_in(rest(slice(n, 2 * n)), vr_sem, gc[1])
+    all_in(rest(slice(0, n)), fr, gc[1])
+
+    avr[...] = mm(yw[:, 0:n], l2i, NT) + yw[:, n:]
+    late.start_one()
     vr = mm(lead_ref[:, 0:n], l2i, NT) + jnp.where(eyes((height, n), row * height), 1.0, 0.0)
+    src3[...] = mm(vr, avr[...], TN)
+    red = Reduce(out3, red3[0], red3[1], red3[2:], ncol)
+    red.start_first(src3)
     with_identity(work, mm(xt, l2i, NT).T + jnp.where(eyes((n, n)), 1.0, 0.0))
-    for j in range(4):
+    near = (1, 3)
+    gj_inverse(work, {4: red.start_second, 6: lambda: late.forward(0, near)})
+    k = work[:, n:]
+
+    def vectors(j):
         shift = (c * 4 + j) * height
         vc_ref[j] = mm(vc_ref[j], l2i, NT) + jnp.where(eyes((height, n), shift), 1.0, 0.0)
         put(vc_ref.at[j], vc_out.at[j])
-    all_in(rest(slice(n, 2 * n)), vr_sem, gc[1])
-    all_in(rest(slice(0, n)), fr, gc[1])
-
-    avr[...] = mm(yw[:, 0:n], l2i, NT) + yw[:, n:]
-    late.start_one()
-    src3[...] = mm(vr, avr[...], TN)
-    red = Reduce(out3, red3[0], red3[1], red3[2:], ncol)
-    red.start_x(src3)
-    near = (1, 3)
-    gj_inverse(work, {4: red.start_z, 6: lambda: late.forward(0, near)})
-    k = work[:, n:]
-    for j in range(1, 4):
-        late.forward(j, near)
+
+    late.forward(1, near)
     red.start_c()
+    late.forward(2, near)
+    late.forward(3, near)
+    vectors(0)
     late.relay(0)
+    vectors(1)
     late.relay(1)
+    vectors(2)
+    late.relay(2)
+    vectors(3)
     band_ref[...] = -mm(l2, l1_ref[...], (((0,), (1,)), ((), ())))
     put(band_ref, band_out)
-    late.relay(2)
     late.relay(3)
     red.finish()
     inner = mm(k, mm(out3[...], k), TN)

time: 88.9 us -> 84.7 us (0.953)
  Pallas kernels: 87.9 us -> 83.8 us
    pallas_call x1, Pallas kernels: 80.9 us -> 76.8 us  [body(): pl.pallas_call(functools.partial(main_kernel, ncol), out_shape=(struct(n,...]
where the time goes in v5:
time: 84.7 us; the launch traced here: 84.6 us
  Pallas kernels  83.8 us (99%)
    pallas_call x1, Pallas kernels, body(): pl.pallas_call(functools.partial(main_kernel, ncol), out_shape=(struct(n,...  76.8 us
    pallas_call x1, Pallas kernels, body(): pl.pallas_call(last_kernel, out_shape=(struct(height, width), struct(n, n...  6.99 us

profile of v5, /device:TPU:1, one launch (start us, length us, event | category | flops | bytes accessed | tf_op | source)
XLA Modules:
  0.0 84.6 jit_solution(18394568560344637934)
XLA Ops:
  0.6 76.8 %main.1 = (f32[128,128]{1,0:T(8,128)}, f32[128,128]{1,0:T(8,128)}, f32[512,256]{1,0:T(8,128)}, f32[4,512,128]{2,1,0:T(8,128)}, f32[4,512,128]{2,1,0:T(8,128)}) custom-call(f32[512,128]{1,0:T(8,128)} %p_hbm.1, f32[512,2048]{1,0:T(8,128)} %a_ref.3), custom_call_target="tpu_custom_call" | custom-call | tf_op jit(solution)/shard_map/main/pallas_call | solution.py:496
  77.4 7.0 %last.1 = (f32[512,2048]{1,0:T(8,128)}, f32[128,128]{1,0:T(8,128)}, f32[128,128]{1,0:T(8,128)}) custom-call(f32[128,128]{1,0:T(8,128)} %get-tuple-element.8.l1_in, f32[128,128]{1,0:T(8,128)} %get-tuple-element.9.band_in, f32[512,256]{1,0:T(8,128)} %get-tuple-element.10.lead_ref, f32[4,512,128]{2,1,0:T(8,128)} %get-tuple-element.11.avc_ref, ...), custom_call_target="tpu_custom_call" | custom-call | tf_op jit(solution)/shard_map/last/pallas_call | solution.py:509

commit v6 on v5

--- a/solution.py
+++ b/solution.py
@@ -205,7 +205,7 @@
 
 
 def comm_params(cid):
-    return pltpu.CompilerParams(collective_id=cid, has_side_effects=True, vmem_limit_bytes=60 << 20)
+    return pltpu.CompilerParams(collective_id=cid, has_side_effects=True, vmem_limit_bytes=32 << 20)
 
 
 def turn(y):
@@ -284,7 +284,7 @@
     return jax.ShapeDtypeStruct(shape, F32)
 
 
-def main_kernel(ncol, p_hbm, a_ref, l1_out, band_out, lead_out, avc_out, vc_out, *scratch):
+def main_kernel(ncol, p_hbm, a_ref, l1_ref, band_ref, lead_ref, avc_ref, vc_ref, av, *scratch):
     scratch = list(scratch)
 
     def take(count):
@@ -295,9 +295,9 @@
     src1, out1, src2, out2, src3, out3 = take(6)
     red1, red2, red3 = take(8), take(8), take(8)
     gs1, gs2 = take(6), take(6)
-    av, pc, work, rows, yp, ybuf, wbuf, yw, avr = take(9)
-    p_ref, l1_ref, band_ref, lead_ref, avc_ref, vc_ref = take(6)
-    asem, psem, osem, ys, yr, ws, wr, vs, vr_sem, fs, fr = take(11)
+    pc, work, rows, yp, ybuf, wbuf, yw, avr = take(8)
+    p_ref, = take(1)
+    asem, psem, ys, yr, ws, wr, vs, vr_sem, fs, fr = take(10)
     n = p_ref.shape[1]
     height = p_ref.shape[0]
     sl = height // ncol
@@ -313,13 +313,6 @@
     fetch.start()
     load = pltpu.make_async_copy(a_ref, av, asem)
     load.start()
-    outs = []
-
-    def put(src, dst):
-        copy = pltpu.make_async_copy(src, dst, osem.at[len(outs)])
-        copy.start()
-        outs.append(copy)
-
     fetch.wait()
     p = p_ref[...]
     src1[0:n, :] = mm(p, p, TN)
@@ -369,7 +362,6 @@
     red = Reduce(out2, red2[1], red2[0], red2[2:], ncol, z_first=True)
     red.start_first(src2)
     l1_ref[...] = l1
-    put(l1_ref, l1_out)
     lead_ref[:, 0:n] = xr
     xt = mm(out1[n:, :], l1i, NT)
 
@@ -424,7 +416,6 @@
     def vectors(j):
         shift = (c * 4 + j) * height
         vc_ref[j] = mm(vc_ref[j], l2i, NT) + jnp.where(eyes((height, n), shift), 1.0, 0.0)
-        put(vc_ref.at[j], vc_out.at[j])
 
     late.forward(1, near)
     red.start_c()
@@ -438,7 +429,6 @@
     late.relay(2)
     vectors(3)
     band_ref[...] = -mm(l2, l1_ref[...], (((0,), (1,)), ((), ())))
-    put(band_ref, band_out)
     late.relay(3)
     red.finish()
     inner = mm(k, mm(out3[...], k), TN)
@@ -446,14 +436,9 @@
         jnp.concatenate([jnp.zeros((n, n), F32), k], axis=1),
         jnp.concatenate([k.T, -0.5 * (inner + inner.T)], axis=1)], axis=0)
     lead_ref[...] = mm(jnp.concatenate([avr[...], vr], axis=1), right)
-    put(lead_ref, lead_out)
     for j in range(4):
-        at = late.nearest(j)
-        late.relayed(at)
-        put(avc_ref.at[at], avc_out.at[at])
+        late.relayed(late.nearest(j))
     late.finish(2)
-    for copy in outs:
-        copy.wait()
     all_out(ybuf.at[1:ncol], ys, gc[1])
     all_out(rest(slice(0, n)), fs, gc[1])
     all_out(rest(slice(n, 2 * n)), vs, gc[1])
@@ -463,23 +448,19 @@
         all_out(rest(slice(0, n)), ws, gc[1])
 
 
-def last_kernel(l1_in, band_in, lead_ref, avc_ref, vc_ref, a_ref, out_ref, band_ref, l1_ref, abuf, obuf, insem, outsem):
+def last_kernel(l1_in, band_in, lead_ref, avc_ref, vc_ref, a_ref, out_ref, band_ref, l1_ref, obuf, outsem):
     width = avc_ref.shape[1]
-    loads = [pltpu.make_async_copy(a_ref.at[:, k * width:(k + 1) * width], abuf.at[k], insem.at[k]) for k in range(4)]
-    for copy in loads:
-        copy.start()
-    band_ref[...] = band_in[...]
-    l1_ref[...] = l1_in[...]
     lead = halves(lead_ref[...])
     stores = []
     for k in range(4):
+        cols = slice(k * width, (k + 1) * width)
         tail = halves(jnp.concatenate([avc_ref[k], vc_ref[k]], axis=1))
-        prod = mm3(lead, tail, NT)
-        loads[k].wait()
-        obuf[k] = abuf[k] - prod
-        copy = pltpu.make_async_copy(obuf.at[k], out_ref.at[:, k * width:(k + 1) * width], outsem.at[k])
+        obuf[k] = a_ref[:, cols] - mm3(lead, tail, NT)
+        copy = pltpu.make_async_copy(obuf.at[k], out_ref.at[:, cols], outsem.at[k])
         copy.start()
         stores.append(copy)
+    band_ref[...] = band_in[...]
+    l1_ref[...] = l1_in[...]
     for copy in stores:
         copy.wait()
 
@@ -493,25 +474,25 @@
     def vmem(*shape):
         return pltpu.VMEM(shape, F32)
 
-    l1, band, lead, avc, vc = pl.pallas_call(
+    l1, band, lead, avc, vc, kept = pl.pallas_call(
         functools.partial(main_kernel, ncol),
-        out_shape=(struct(n, n), struct(n, n), struct(height, 2 * n), struct(4, height, n), struct(4, height, n)),
-        in_specs=[ANY, ANY], out_specs=(ANY,) * 5,
+        out_shape=(vmem(n, n), vmem(n, n), vmem(height, 2 * n), vmem(4, height, n), vmem(4, height, n), vmem(height, width)),
+        in_specs=[ANY, ANY], out_specs=(VM,) * 6,
         scratch_shapes=[vmem(2 * n, n), vmem(2 * n, n), vmem(n, n), vmem(n, n), vmem(n, n), vmem(n, n)]
         + reduce_scratch(2 * n, ncol) + reduce_scratch(n, ncol) + reduce_scratch(n, ncol)
         + gather_sems() + gather_sems()
-        + [vmem(height, width), vmem(4, height, n), vmem(n, 2 * n), vmem(n, 2 * n), vmem(height, n),
+        + [vmem(4, height, n), vmem(n, 2 * n), vmem(n, 2 * n), vmem(height, n),
            vmem(ncol, sl, n), vmem(sl, n), vmem(height, 2 * n), vmem(height, n),
-           vmem(height, n), vmem(n, n), vmem(n, n), vmem(height, 2 * n), vmem(4, height, n), vmem(4, height, n)]
-        + [dma, dma, dma((11,)), dma, dma, dma, dma, dma, dma, dma, dma],
-        compiler_params=pltpu.CompilerParams(collective_id=0, has_side_effects=True, vmem_limit_bytes=60 << 20),
+           vmem(height, n)]
+        + [dma, dma, dma, dma, dma, dma, dma, dma, dma, dma],
+        compiler_params=pltpu.CompilerParams(collective_id=0, has_side_effects=True, vmem_limit_bytes=56 << 20),
         name="main")(panel, trailing)
     reduced, band, l1 = pl.pallas_call(
         last_kernel, out_shape=(struct(height, width), struct(n, n), struct(n, n)),
-        in_specs=[VM] * 5 + [ANY], out_specs=(ANY, VM, VM),
-        scratch_shapes=[vmem(4, height, width // 4), vmem(4, height, width // 4), dma((4,)), dma((4,))],
-        compiler_params=pltpu.CompilerParams(vmem_limit_bytes=60 << 20), name="last",
-    )(l1, band, lead, avc, vc, trailing)
+        in_specs=[VM] * 6, out_specs=(ANY, VM, VM),
+        scratch_shapes=[vmem(4, height, width // 4), dma((4,))],
+        compiler_params=pltpu.CompilerParams(vmem_limit_bytes=32 << 20), name="last",
+    )(l1, band, lead, avc, vc, kept)
     return reduced, band, l1
 
 

time: 84.7 us -> 80.3 us (0.948)
  Pallas kernels: 83.8 us -> 79.5 us
    pallas_call x1, Pallas kernels: 6.99 us -> 3.5 us  [body(): pl.pallas_call(last_kernel, out_shape=(struct(height, width), struct(n, n...]
where the time goes in v6:
time: 80.3 us
  Pallas kernels  79.5 us (99%)
    pallas_call x1, Pallas kernels, body(): pl.pallas_call(functools.partial(main_kernel, ncol), out_shape=(vmem(n, n...  76 us
    pallas_call x1, Pallas kernels, body(): pl.pallas_call(last_kernel, out_shape=(struct(height, width), struct(n, n...  3.5 us

profile of v6, /device:TPU:1, one launch (start us, length us, event | category | flops | bytes accessed | tf_op | source)
XLA Modules:
  0.0 80.3 jit_solution(17249002821069679937)
XLA Ops:
  0.6 76.0 %main.1 = (f32[128,128]{1,0:T(8,128)S(1)}, f32[128,128]{1,0:T(8,128)S(1)}, f32[512,256]{1,0:T(8,128)S(1)}, f32[4,512,128]{2,1,0:T(8,128)S(1)}, f32[4,512,128]{2,1,0:T(8,128)S(1)}, /*index=5*/f32[512,2048]{1,0:T(8,128)S(1)}) custom-call(f32[512,128]{1,0:T(8,128)} %p_hbm.1, f32[512,2048]{1,0:T(8,128)} %a_ref.1), custom_call_target="tpu_custom_call" | custom-call | tf_op jit(solution)/shard_map/main/pallas_call | solution.py:477
  76.6 3.5 %last.1 = (f32[512,2048]{1,0:T(8,128)}, f32[128,128]{1,0:T(8,128)}, f32[128,128]{1,0:T(8,128)}) custom-call(f32[128,128]{1,0:T(8,128)S(1)} %get-tuple-element.9.l1_in, f32[128,128]{1,0:T(8,128)S(1)} %get-tuple-element.10.band_in, f32[512,256]{1,0:T(8,128)S(1)} %get-tuple-element.11.lead_ref, f32[4,512,128]{2,1,0:T(8,128)S(1)} %get-tuple-element.12.avc_ref, ...), custom_call_target="tpu_custom_call" | custom-call | tf_op jit(solution)/shard_map/last/pallas_call | solution.py:490

commit v7 on v6

--- a/solution.py
+++ b/solution.py
@@ -325,8 +325,6 @@
     red.start_second()
     early.start_one()
     red.start_c()
-    for j in range(4):
-        early.forward(j)
     red.finish()
 
     def part(d):
@@ -354,7 +352,7 @@
         wbuf[...] = av[0:sl, 0:n]
 
     with_identity(work, out1[0:n, :])
-    chol_inv(work, rows)
+    chol_inv(work, rows, {j: functools.partial(early.forward, j) for j in range(4)})
     l1, l1i = factors(rows)
 
     xr = mm(p_ref[...], l1i, NT)
@@ -371,24 +369,25 @@
 
     yw[part(0), n:] = wbuf[...]
     share(slice(n, 2 * n), vs, vr_sem)
-    red.start_second()
-
-    def block(k):
+
+    def block(j):
+        k = early.nearest(j)
         early.block(k)
         xk = mm(pc[k], l1i, NT)
         vc_ref[k] = xk
-        return mm3(halves(av[:, k * height:(k + 1) * height]), halves(xk))
+        return mm3(halves(av[:, pl.ds(pl.multiple_of(k * height, 128), height)]), halves(xk))
 
     acc = block(0)
     acc = acc + block(1)
+    red.start_second()
     acc = acc + block(2)
-    red.start_c()
     acc = acc + block(3)
     yp[...] = acc
-    early.finish(3)
+    red.start_c()
     ybuf[0] = yp[part(0), :]
     for d in range(1, ncol):
         send(yp.at[part(d), :], ybuf.at[d], ys, yr, gc[d])
+    early.finish(3)
     red.finish()
 
     def spread():

time: 80.3 us -> 81.1 us (level); the launches traced: 80.3 us -> 80.1 us
  no operation moved by 1% of the time
where the time goes in v7:
time: 81.1 us; the launch traced here: 80.1 us
  Pallas kernels  79.3 us (98%)
    pallas_call x1, Pallas kernels, body(): pl.pallas_call(functools.partial(main_kernel, ncol), out_shape=(vmem(n, n...  75.8 us
    pallas_call x1, Pallas kernels, body(): pl.pallas_call(last_kernel, out_shape=(struct(height, width), struct(n, n...  3.5 us

profile of v7, /device:TPU:1, one launch (start us, length us, event | category | flops | bytes accessed | tf_op | source)
XLA Modules:
  0.0 80.1 jit_solution(13027725809566791453)
XLA Ops:
  0.6 75.8 %main.1 = (f32[128,128]{1,0:T(8,128)S(1)}, f32[128,128]{1,0:T(8,128)S(1)}, f32[512,256]{1,0:T(8,128)S(1)}, f32[4,512,128]{2,1,0:T(8,128)S(1)}, f32[4,512,128]{2,1,0:T(8,128)S(1)}, /*index=5*/f32[512,2048]{1,0:T(8,128)S(1)}) custom-call(f32[512,128]{1,0:T(8,128)} %p_hbm.1, f32[512,2048]{1,0:T(8,128)} %a_ref.1), custom_call_target="tpu_custom_call" | custom-call | tf_op jit(solution)/shard_map/main/pallas_call | solution.py:476
  76.5 3.5 %last.1 = (f32[512,2048]{1,0:T(8,128)}, f32[128,128]{1,0:T(8,128)}, f32[128,128]{1,0:T(8,128)}) custom-call(f32[128,128]{1,0:T(8,128)S(1)} %get-tuple-element.9.l1_in, f32[128,128]{1,0:T(8,128)S(1)} %get-tuple-element.10.band_in, f32[512,256]{1,0:T(8,128)S(1)} %get-tuple-element.11.lead_ref, f32[4,512,128]{2,1,0:T(8,128)S(1)} %get-tuple-element.12.avc_ref, ...), custom_call_target="tpu_custom_call" | custom-call | tf_op jit(solution)/shard_map/last/pallas_call | solution.py:489

commit v8 on v6

--- a/solution.py
+++ b/solution.py
@@ -325,8 +325,6 @@
     red.start_second()
     early.start_one()
     red.start_c()
-    for j in range(4):
-        early.forward(j)
     red.finish()
 
     def part(d):
@@ -354,7 +352,7 @@
         wbuf[...] = av[0:sl, 0:n]
 
     with_identity(work, out1[0:n, :])
-    chol_inv(work, rows)
+    chol_inv(work, rows, {j: functools.partial(early.forward, j) for j in range(4)})
     l1, l1i = factors(rows)
 
     xr = mm(p_ref[...], l1i, NT)

time: 80.3 us -> 81.6 us (1.016)
  the two profiles are of different devices: /device:TPU:1 before, /device:TPU:81 now
where the time goes in v8:
time: 81.6 us; the launch traced here: 81.5 us
  Pallas kernels  80.7 us (99%)
    pallas_call x1, Pallas kernels, body(): pl.pallas_call(functools.partial(main_kernel, ncol), out_shape=(vmem(n, n...  77.2 us
    pallas_call x1, Pallas kernels, body(): pl.pallas_call(last_kernel, out_shape=(struct(height, width), struct(n, n...  3.5 us

profile of v8, /device:TPU:81, one launch (start us, length us, event | category | flops | bytes accessed | tf_op | source)
XLA Modules:
  0.0 81.5 jit_solution(4098652329636884276)
XLA Ops:
  0.6 77.2 %main.1 = (f32[128,128]{1,0:T(8,128)S(1)}, f32[128,128]{1,0:T(8,128)S(1)}, f32[512,256]{1,0:T(8,128)S(1)}, f32[4,512,128]{2,1,0:T(8,128)S(1)}, f32[4,512,128]{2,1,0:T(8,128)S(1)}, /*index=5*/f32[512,2048]{1,0:T(8,128)S(1)}) custom-call(f32[512,128]{1,0:T(8,128)} %p_hbm.1, f32[512,2048]{1,0:T(8,128)} %a_ref.1), custom_call_target="tpu_custom_call" | custom-call | tf_op jit(solution)/shard_map/main/pallas_call | solution.py:475
  77.8 3.5 %last.1 = (f32[512,2048]{1,0:T(8,128)}, f32[128,128]{1,0:T(8,128)}, f32[128,128]{1,0:T(8,128)}) custom-call(f32[128,128]{1,0:T(8,128)S(1)} %get-tuple-element.9.l1_in, f32[128,128]{1,0:T(8,128)S(1)} %get-tuple-element.10.band_in, f32[512,256]{1,0:T(8,128)S(1)} %get-tuple-element.11.lead_ref, f32[4,512,128]{2,1,0:T(8,128)S(1)} %get-tuple-element.12.avc_ref, ...), custom_call_target="tpu_custom_call" | custom-call | tf_op jit(solution)/shard_map/last/pallas_call | solution.py:488
